TPU v7x, 32 devices: a whole 2x2x4 slice. The times are simulated.
32 devices in a mesh: dp: 8 (over y, x, core), tensor: 4 (over z).
Axes of the slice: x: 2, y: 2, z: 4, core: 2. Of those that a mesh axis runs over, the one named last changes fastest.
Arguments:
- hidden_in: bfloat16 [16384, 1024], P('dp'), may hold values from -6 to 6
- lengths: int32 [8], P('dp'), may hold values from 512 to 2048, as said below
- query_weight: bfloat16 [1024, 1024], P(None, 'tensor'), may hold values from -0.1875 to 0.1875
- query_bias: bfloat16 [1024], P('tensor'), may hold values from -1 to 1
- key_weight: bfloat16 [1024, 1024], P(None, 'tensor'), may hold values from -0.1875 to 0.1875
- value_weight: bfloat16 [1024, 1024], P(None, 'tensor'), may hold values from -0.1875 to 0.1875
- value_bias: bfloat16 [1024], P('tensor'), may hold values from -1 to 1
- output_weight: bfloat16 [1024, 1024], P(None, 'tensor'), may hold values from -2 to 2
- output_bias: bfloat16 [1024], replicated, may hold values from -1 to 1
- first_gain: bfloat16 [1024], replicated, may hold values from 0.5 to 1.5
- first_shift: bfloat16 [1024], replicated, may hold values from -1 to 1
- inner_weight: bfloat16 [1024, 4096], P(None, 'tensor'), may hold values from -0.1875 to 0.1875
- inner_bias: bfloat16 [4096], P('tensor'), may hold values from -1 to 1
- outer_weight: bfloat16 [1024, 4096], P(None, 'tensor'), may hold values from -0.125 to 0.125
- outer_bias: bfloat16 [1024], replicated, may hold values from -1 to 1
- second_gain: bfloat16 [1024], replicated, may hold values from 0.5 to 1.5
- second_shift: bfloat16 [1024], replicated, may hold values from -1 to 1
- cotangent: bfloat16 [16384, 1024], P('dp'), may hold values from -6 to 6
- teacher: bfloat16 [16384, 1024], P('dp'), may hold values from -6 to 6
Outputs:
- layer_output: bfloat16 [16384, 1024], P(('dp', 'tensor'))
- distill_loss: float32 [], replicated
- input_grad: float32 [16384, 1024], P(('dp', 'tensor'))
- query_weight_grad: float32 [1024, 1024], P('dp', 'tensor')
- query_bias_grad: float32 [1024], replicated
- key_weight_grad: float32 [1024, 1024], P('dp', 'tensor')
- value_weight_grad: float32 [1024, 1024], P('dp', 'tensor')
- value_bias_grad: float32 [1024], replicated
- output_weight_grad: float32 [1024, 1024], P('dp', 'tensor')
- output_bias_grad: float32 [1024], replicated
- first_gain_grad: float32 [1024], replicated
- first_shift_grad: float32 [1024], replicated
- inner_weight_grad: float32 [1024, 4096], P('dp', 'tensor')
- inner_bias_grad: float32 [4096], replicated
- outer_weight_grad: float32 [1024, 4096], P('dp', 'tensor')
- outer_bias_grad: float32 [1024], replicated
- second_gain_grad: float32 [1024], replicated
- second_shift_grad: float32 [1024], replicated
Inputs may be any that keep to these rules, and one draw needn't show every extreme that they name: `lengths`: one sequence's valid tokens; slots after them are padding; some sequence fills all 2048 slots.
All inputs are finite; a program needn't handle non-finite values.
Results may differ from a plain program's by a relative error of at most 0.018.
Values may be sent and summed in bfloat16 or wider, within the bound.
No kernel may reach another device: no remote copies, remote signals or barrier semaphores. Data moves between devices by JAX's collectives and lax.ppermute only.
A program may use at most 256 MiB of HBM per device.

v0:
```python
import math

import jax
import jax.numpy as jnp
from jax import lax
from jax.sharding import PartitionSpec as P

HD = 64


epsilon = 1e-05


def matmul(former, latter):
    return jnp.dot(former, latter, preferred_element_type=jnp.float32)


def times_rows(former, latter):
    return lax.dot_general(
        former, latter, (((1,), (1,)), ((), ())), preferred_element_type=jnp.float32
    )


def over_rows(former, latter):
    return lax.dot_general(
        former, latter, (((0,), (0,)), ((), ())), preferred_element_type=jnp.float32
    )


def layer_norm(hidden, norm_gain, norm_shift):
    centered = hidden - jnp.mean(hidden, axis=-1, keepdims=True)
    inverse = lax.rsqrt(jnp.mean(centered * centered, axis=-1, keepdims=True) + epsilon)
    normal = centered * inverse
    return (normal * norm_gain + norm_shift, normal, inverse)


def norm_back(upstream, normal, inverse, norm_gain):
    scaled = upstream * norm_gain
    return inverse * (
        scaled
        - jnp.mean(scaled, axis=-1, keepdims=True)
        - normal * jnp.mean(scaled * normal, axis=-1, keepdims=True)
    )


def gelu_exact(values):
    return 0.5 * values * (1.0 + jax.scipy.special.erf(values * 0.7071067811865476))


def gelu_slope(values):
    return (
        0.5 * (1.0 + jax.scipy.special.erf(values * 0.7071067811865476))
        + values * jnp.exp(-0.5 * values * values) * 0.3989422804014327
    )


def split_blocks(queries, keys_all, values_all):
    seq_len, local_width = queries.shape
    heads_here = local_width // HD
    block_rows = min(512, seq_len)
    block_count = seq_len // block_rows
    keys_split = keys_all.reshape(seq_len, heads_here, HD)
    values_split = values_all.reshape(seq_len, heads_here, HD)
    query_blocks = queries.reshape(block_count, block_rows, heads_here, HD)
    return (keys_split, values_split, query_blocks, block_count, block_rows, heads_here)


def block_scores(query_block, keys_split, key_valid, score_scale):
    scores = (
        jnp.einsum("qhd,khd->hqk", query_block, keys_split, preferred_element_type=jnp.float32)
        * score_scale
    )
    return jnp.where(key_valid[None, None, :], scores, -1e30)


def attend_forward(queries, keys_all, values_all, key_valid, score_scale):
    keys_split, values_split, query_blocks, block_count, block_rows, heads_here = split_blocks(
        queries, keys_all, values_all
    )

    def one_block(query_block):
        scores = block_scores(query_block, keys_split, key_valid, score_scale)
        row_peak = jnp.max(scores, axis=-1, keepdims=True)
        exponent = jnp.exp(scores - row_peak)
        row_total = jnp.sum(exponent, axis=-1, keepdims=True)
        probs = (exponent / row_total).astype(jnp.bfloat16)
        context = jnp.einsum(
            "hqk,khd->qhd", probs, values_split, preferred_element_type=jnp.float32
        )
        return (context, (row_peak + jnp.log(row_total))[..., 0])

    context, logsum = lax.map(one_block, query_blocks)
    return (context.reshape(queries.shape), logsum)


def attend_backward(queries, keys_all, values_all, key_valid, score_scale, logsum, context_grad):
    keys_split, values_split, query_blocks, block_count, block_rows, heads_here = split_blocks(
        queries, keys_all, values_all
    )
    grad_blocks = context_grad.reshape(block_count, block_rows, heads_here, HD)

    def one_block(carry, inputs):
        key_sum, value_sum = carry
        query_block, grad_block, logsum_block = inputs
        scores = block_scores(query_block, keys_split, key_valid, score_scale)
        probs = jnp.exp(scores - logsum_block[..., None])
        prob_grad = jnp.einsum(
            "qhd,khd->hqk", grad_block, values_split, preferred_element_type=jnp.float32
        )
        centre = jnp.sum(probs * prob_grad, axis=-1, keepdims=True)
        score_grad = (probs * (prob_grad - centre)).astype(jnp.bfloat16)
        query_grad = (
            jnp.einsum("hqk,khd->qhd", score_grad, keys_split, preferred_element_type=jnp.float32)
            * score_scale
        )
        key_sum = (
            key_sum
            + jnp.einsum(
                "hqk,qhd->khd", score_grad, query_block, preferred_element_type=jnp.float32
            )
            * score_scale
        )
        value_sum = value_sum + jnp.einsum(
            "hqk,qhd->khd",
            probs.astype(jnp.bfloat16),
            grad_block,
            preferred_element_type=jnp.float32,
        )
        return ((key_sum, value_sum), query_grad)

    zero_block = jnp.zeros(keys_split.shape, jnp.float32)
    (key_sum, value_sum), query_grads = lax.scan(
        one_block, (zero_block, zero_block), (query_blocks, grad_blocks, logsum)
    )
    return (
        query_grads.reshape(queries.shape),
        key_sum.reshape(queries.shape),
        value_sum.reshape(queries.shape),
    )


def shards(
    hidden_in,
    lengths,
    query_weight,
    query_bias,
    key_weight,
    value_weight,
    value_bias,
    output_weight,
    output_bias,
    first_gain,
    first_shift,
    inner_weight,
    inner_bias,
    outer_weight,
    outer_bias,
    second_gain,
    second_shift,
    cotangent,
    teacher,
):
    seq_len, model_width = hidden_in.shape
    tensor_size = lax.axis_size("tensor")
    tensor_index = lax.axis_index("tensor")
    share_rows = seq_len // tensor_size
    row_start = tensor_index * share_rows
    score_scale = 1.0 / math.sqrt(HD)
    positions = jnp.arange(seq_len, dtype=jnp.int32)
    row_valid = positions < lengths[0]
    token_total = lax.psum(jnp.sum(lengths), "dp").astype(jnp.float32)
    grad_scale = seq_len * lax.axis_size("dp") / (2.0 * token_total)
    hidden_float = hidden_in.astype(jnp.float32)
    queries = (matmul(hidden_in, query_weight) + query_bias).astype(jnp.bfloat16)
    keys_all = matmul(hidden_in, key_weight).astype(jnp.bfloat16)
    values_all = (matmul(hidden_in, value_weight) + value_bias).astype(jnp.bfloat16)
    context, logsum = attend_forward(queries, keys_all, values_all, row_valid, score_scale)
    context_low = context.astype(jnp.bfloat16)
    attention_part = times_rows(context_low, output_weight)

    def take_own(array_in):
        return lax.dynamic_slice_in_dim(array_in, row_start, share_rows, 0)

    attention_whole = lax.psum(attention_part, "tensor")
    normed, normal_one, inverse_one = layer_norm(
        hidden_float + (attention_whole + output_bias), first_gain, first_shift
    )
    normed_low = normed.astype(jnp.bfloat16)
    inner = matmul(normed_low, inner_weight) + inner_bias
    activated = gelu_exact(inner).astype(jnp.bfloat16)
    outer_part = times_rows(activated, outer_weight)
    outer_rows = lax.psum(outer_part, "tensor")
    final, normal_two, inverse_two = layer_norm(
        normed + (outer_rows + outer_bias), second_gain, second_shift
    )
    row_mask = row_valid[:, None]
    difference = final - teacher.astype(jnp.float32)
    loss_part = jnp.sum(take_own(jnp.where(row_mask, difference * difference, 0.0)))
    final_grad = jnp.where(row_mask, cotangent.astype(jnp.float32) + grad_scale * difference, 0.0)
    second_grad = norm_back(final_grad, normal_two, inverse_two, second_gain)
    branch_low = second_grad.astype(jnp.bfloat16)
    activated_grad = matmul(branch_low, outer_weight)
    outer_weight_grad = over_rows(branch_low, activated)
    inner_low = (activated_grad * gelu_slope(inner)).astype(jnp.bfloat16)
    inner_bias_grad = jnp.sum(inner_low.astype(jnp.float32), axis=0)
    inner_weight_grad = over_rows(normed_low, inner_low)
    normed_part = times_rows(inner_low, inner_weight)
    normed_back = lax.psum(normed_part, "tensor")
    normed_grad = second_grad + normed_back
    first_grad = norm_back(normed_grad, normal_one, inverse_one, first_gain)
    attention_low = first_grad.astype(jnp.bfloat16)
    output_weight_grad = over_rows(attention_low, context_low)
    context_grad = matmul(attention_low, output_weight).astype(jnp.bfloat16)
    query_grad, key_grad, value_grad = attend_backward(
        queries, keys_all, values_all, row_valid, score_scale, logsum, context_grad
    )
    query_low = query_grad.astype(jnp.bfloat16)
    key_low = key_grad.astype(jnp.bfloat16)
    value_low = value_grad.astype(jnp.bfloat16)
    input_part = (
        times_rows(query_low, query_weight)
        + times_rows(key_low, key_weight)
        + times_rows(value_low, value_weight)
    )
    input_back = lax.psum(input_part.astype(jnp.bfloat16), "tensor").astype(jnp.float32)
    input_rows = take_own(input_back) + take_own(first_grad)
    weight_grads = (
        lax.psum_scatter(
            over_rows(hidden_in, query_low).astype(jnp.bfloat16),
            "dp",
            scatter_dimension=0,
            tiled=True,
        ).astype(jnp.float32),
        lax.psum_scatter(
            over_rows(hidden_in, key_low).astype(jnp.bfloat16),
            "dp",
            scatter_dimension=0,
            tiled=True,
        ).astype(jnp.float32),
        lax.psum_scatter(
            over_rows(hidden_in, value_low).astype(jnp.bfloat16),
            "dp",
            scatter_dimension=0,
            tiled=True,
        ).astype(jnp.float32),
        lax.psum_scatter(
            output_weight_grad.astype(jnp.bfloat16), "dp", scatter_dimension=0, tiled=True
        ).astype(jnp.float32),
        lax.psum_scatter(
            inner_weight_grad.astype(jnp.bfloat16), "dp", scatter_dimension=0, tiled=True
        ).astype(jnp.float32),
        lax.psum_scatter(
            outer_weight_grad.astype(jnp.bfloat16), "dp", scatter_dimension=0, tiled=True
        ).astype(jnp.float32),
    )

    def placed(vector_in):
        full_zeros = jnp.zeros((vector_in.shape[0] * tensor_size,), jnp.float32)
        return lax.dynamic_update_slice_in_dim(
            full_zeros, vector_in, tensor_index * vector_in.shape[0], 0
        )

    vector_grads = lax.psum(
        (
            placed(jnp.sum(query_low.astype(jnp.float32), axis=0)),
            placed(jnp.sum(value_low.astype(jnp.float32), axis=0)),
            jnp.sum(take_own(attention_low).astype(jnp.float32), axis=0),
            jnp.sum(take_own(normed_grad * normal_one), axis=0),
            jnp.sum(take_own(normed_grad), axis=0),
            placed(inner_bias_grad),
            jnp.sum(take_own(branch_low).astype(jnp.float32), axis=0),
            jnp.sum(take_own(final_grad * normal_two), axis=0),
            jnp.sum(take_own(final_grad), axis=0),
            loss_part,
        ),
        ("dp", "tensor"),
    )
    (
        query_bias_grad,
        value_bias_grad,
        output_bias_grad,
        first_gain_grad,
        first_shift_grad,
        inner_bias_full,
        outer_bias_grad,
        second_gain_grad,
        second_shift_grad,
        loss_total,
    ) = vector_grads
    (
        query_weight_grad,
        key_weight_grad,
        value_weight_grad,
        output_weight_sum,
        inner_weight_sum,
        outer_weight_sum,
    ) = weight_grads
    distill_loss = loss_total / token_total
    return (
        take_own(final).astype(jnp.bfloat16),
        distill_loss,
        input_rows,
        query_weight_grad,
        query_bias_grad,
        key_weight_grad,
        value_weight_grad,
        value_bias_grad,
        output_weight_sum,
        output_bias_grad,
        first_gain_grad,
        first_shift_grad,
        inner_weight_sum,
        inner_bias_full,
        outer_weight_sum,
        outer_bias_grad,
        second_gain_grad,
        second_shift_grad,
    )


def solution(mesh):
    in_specs = (
        P("dp", None),
        P("dp"),
        P(None, "tensor"),
        P("tensor"),
        P(None, "tensor"),
        P(None, "tensor"),
        P("tensor"),
        P(None, "tensor"),
        P(),
        P(),
        P(),
        P(None, "tensor"),
        P("tensor"),
        P(None, "tensor"),
        P(),
        P(),
        P(),
        P("dp", None),
        P("dp", None),
    )
    out_specs = (
        P(("dp", "tensor"), None),
        P(),
        P(("dp", "tensor"), None),
        P("dp", "tensor"),
        P(),
        P("dp", "tensor"),
        P("dp", "tensor"),
        P(),
        P("dp", "tensor"),
        P(),
        P(),
        P(),
        P("dp", "tensor"),
        P(),
        P("dp", "tensor"),
        P(),
        P(),
        P(),
    )
    return jax.shard_map(shards, mesh=mesh, in_specs=in_specs, out_specs=out_specs, check_vma=False)
```

profile of v0, /device:TPU:0, one launch (start us, length us, event | category | flops | bytes accessed | tf_op | source)
XLA Modules:
  0.0 1564.1 jit_solution(17279428161375169190)
XLA Ops:
  25.2 55.2 %while.28 = (s32[]{:T(128)}, bf16[4,512,4,64]{1,3,2,0:T(8,128)(2,1)}, f32[4,4,512]{2,1,0:T(4,128)S(1)}, bf16[4,512,4,64]{1,3,2,0:T(8,128)(2,1)}, bf16[2048,4,64]...) while((s32[]{:T(128)}, bf16[4,512,4,64]{1,3,2,0:T(8,128)(2,1)}, ...), condition=%wide.region_3.4_spmd.clone, body=%wide.region_0.3_spmd.clone.sunk | while | flops 1124073472 | bytes 65872064 | solution.py:92
  89.8 293.4 %all-reduce.6.cloned.1.call-done = f32[2048,1024]{1,0:T(8,128)} async-done(((f32[2048,1024]{1,0:T(8,128)}), f32[2048,1024]{1,0:T(8,128)}) %all-reduce.6.cloned.1.call-update) | async-done | bytes 8388624 | tf_op jit(solution)/shard_map/psum | solution.py:184
  421.3 279.7 %all-reduce.8.cloned.1.call-done = f32[2048,1024]{1,0:T(8,128)} async-done(((f32[2048,1024]{1,0:T(8,128)}), f32[2048,1024]{1,0:T(8,128)}) %all-reduce.8.cloned.1.call-update) | async-done | bytes 8388624 | tf_op jit(solution)/shard_map/psum | solution.py:192
  708.8 10.9 multiply_reduce_fusion.6
  725.8 11.3 convert_reduce_fusion
  746.5 9.4 convolution_convert_fusion.2
  756.0 10.5 convolution_convert_fusion.3
  766.7 269.2 %all-reduce.10.cloned.1.call-done = f32[2048,1024]{1,0:T(8,128)} async-done(((f32[2048,1024]{1,0:T(8,128)}), f32[2048,1024]{1,0:T(8,128)}) %all-reduce.10.cloned.1.call-update) | async-done | bytes 8388624 | tf_op jit(solution)/shard_map/psum | solution.py:208
  1036.0 16.3 %multiply_reduce_fusion.5 = (f32[2048]{0:T(1024)S(1)}, f32[2048]{0:T(1024)S(1)}, f32[2048,1024]{1,0:T(8,128)}) fusion(f32[1024]{0:T(1024)S(1)} %convert_element_type.183, f32[2048,1024]{1,0:T(8,128)} %copy-done.5, f32[2048,1024]{1,0:T(8,128)} %all-reduce.10.cloned.1.call-done, f32[2048,1024]{1,0:T(8,128)} %copy-done.7, f32[2048]{0:T(1024)S(1)} %get-tuple-element.345, ...), kind=kLoop, calls=%fused_computation.76 | loop fusion | flops 20967424 | bytes 41992192 | tf_op jit(solution)/shard_map/reduce_sum | solution.py:41
  1052.4 9.8 fusion.67
  1076.0 166.5 %while.29 = (s32[]{:T(128)}, f32[2048,4,64]{0,2,1:T(8,128)S(1)}, f32[2048,4,64]{0,2,1:T(8,128)}, bf16[4,512,4,64]{1,3,2,0:T(8,128)(2,1)}, bf16[4,512,4,64]{1,3,2...) while((s32[]{:T(128)}, f32[2048,4,64]{0,2,1:T(8,128)S(1)}, ...), condition=%wide.region_20.21_spmd.clone, body=%wide.region_18.20_spmd.clone.sunk | while | flops 2750021632 | bytes 180945136 | solution.py:132
  1086.7 10.1 multiply_reduce_fusion.8
  1096.8 11.0 multiply_convert_fusion.3
  1128.8 9.9 multiply_reduce_fusion.8
  1138.7 10.6 multiply_convert_fusion.3
  1170.2 9.9 multiply_reduce_fusion.8
  1180.1 10.6 multiply_convert_fusion.3
  1211.7 9.9 multiply_reduce_fusion.8
  1221.6 10.6 multiply_convert_fusion.3
  1277.1 9.1 add_convert_fusion
  1304.3 40.3 %all-reduce = (f32[]{:T(128)}, f32[1024]{0:T(1024)}, f32[1024]{0:T(1024)}, f32[1024]{0:T(1024)}, f32[1024]{0:T(1024)}, /*index=5*/f32[1024]{0:T(1024)}, f32[4096...) all-reduce(f32[]{:T(128)} %get-tuple-element.344, ...), channel_id=1, replica_groups=mesh['dp'=8,'tensor'=4] {'dp','tensor'}, use_global_device_ids=true, to_apply=%region_11.12 | all-reduce | flops 12289 | bytes 98312 | tf_op jit(solution)/shard_map/psum | solution.py:263
  1348.7 8.8 reduce-scatter.23.cloned.1.call-done
  1359.3 35.5 %reduce-scatter.13.cloned.1.call-done = bf16[128,256]{1,0:T(8,128)(2,1)} async-done(((bf16[1024,256]{1,0:T(8,128)(2,1)}), bf16[128,256]{1,0:T(8,128)(2,1)}) %reduce-scatter.13.cloned.1.call-update) | async-done | bytes 65552 | tf_op jit(solution)/shard_map/reduce_scatter | solution.py:246
  1396.3 155.7 %all-reduce.12.cloned.1.call-done = bf16[2048,1024]{1,0:T(8,128)(2,1)} async-done(((bf16[2048,1024]{1,0:T(8,128)(2,1)}), bf16[2048,1024]{1,0:T(8,128)(2,1)}) %all-reduce.12.cloned.1.call-update) | async-done | bytes 4194320 | tf_op jit(solution)/shard_map/psum | solution.py:225
  (265 shorter events, 302.3 us)
Async XLA Ops:
  7.2 387.5 %copy-start = (bf16[1024,1024]{1,0:T(8,128)(2,1)S(1)}, bf16[1024,1024]{1,0:T(8,128)(2,1)}, u32[]{:S(2)}) copy-start(bf16[1024,1024]{1,0:T(8,128)(2,1)} %param.34) | copy-start | bytes 6291460
  7.2 376.0 %all-reduce.6.cloned.1.call-start = ((), (), s32[]{:S(2)}) async-start(), calls=%async_computation.6 | async-start | bytes 16777216 | tf_op jit(solution)/shard_map/psum | solution.py:184
  89.5 611.5 %all-reduce.8.cloned.1.call-start = ((), (), s32[]{:S(2)}) async-start(), calls=%async_computation.7 | async-start | bytes 16777216 | tf_op jit(solution)/shard_map/psum | solution.py:192
  383.2 8.2 copy-start.10
  394.7 7.4 copy-start.5
  394.8 9.3 copy-start.36
  411.0 10.2 copy-start.33
  411.0 10.2 copy-start.34
  411.0 10.2 copy-start.35
  411.0 625.0 %all-reduce.10.cloned.1.call-start = ((), (), s32[]{:S(2)}) async-start(), calls=%async_computation.8 | async-start | bytes 16777216 | tf_op jit(solution)/shard_map/psum | solution.py:208
  421.3 287.5 %copy-start.27 = (pred[2048]{0:T(1024)(128)(4,1)}, pred[2048]{0:T(1024)(128)(4,1)S(1)}, u32[]{:S(2)}) copy-start(pred[2048]{0:T(1024)(128)(4,1)S(1)} %iota_compare_fusion.2) | copy-start | bytes 6148
  725.8 11.3 copy-start.13
  746.0 549.9 %reduce-scatter.17.cloned.1.call-start = ((), (), s32[]{:S(2)}) async-start(), calls=%async_computation.12 | async-start | bytes 2359296 | tf_op jit(solution)/shard_map/reduce_scatter | solution.py:252
  756.0 541.7 %reduce-scatter.15.cloned.1.call-start = ((), (), s32[]{:S(2)}) async-start(), calls=%async_computation.11 | async-start | bytes 2359296 | tf_op jit(solution)/shard_map/reduce_scatter | solution.py:249
  766.5 578.7 %reduce-scatter.19.cloned.1.call-start = ((), (), s32[]{:S(2)}) async-start(), calls=%async_computation.13 | async-start | bytes 589824
  1052.3 11.8 copy-start.23
  1250.3 96.8 %reduce-scatter.21.cloned.1.call-start = ((), (), s32[]{:S(2)}) async-start(), calls=%async_computation.14 | async-start | bytes 589824
  1256.8 100.8 %reduce-scatter.23.cloned.1.call-start = ((), (), s32[]{:S(2)}) async-start(), calls=%async_computation.15 | async-start | bytes 589824
  1262.3 10.2 copy-start.18
  1267.9 126.8 %reduce-scatter.13.cloned.1.call-start = ((), (), s32[]{:S(2)}) async-start(), calls=%async_computation.10 | async-start | bytes 589824 | tf_op jit(solution)/shard_map/reduce_scatter | solution.py:246
  1277.0 10.1 copy-start.28
  1277.0 275.0 %all-reduce.12.cloned.1.call-start = ((), (), s32[]{:S(2)}) async-start(), calls=%async_computation.9 | async-start | bytes 8388608 | tf_op jit(solution)/shard_map/psum | solution.py:225
  1286.2 13.3 copy-start.12
  1291.3 264.3 %copy-start.1 = (bf16[1024,1024]{1,0:T(8,128)(2,1)S(1)}, bf16[1024,1024]{1,0:T(8,128)(2,1)}, u32[]{:S(2)}) copy-start(bf16[1024,1024]{1,0:T(8,128)(2,1)} %param.34) | copy-start | bytes 6291460
  (44 other events, 161.6 us)
Sparse Core Ops, SparseCore 0:
  89.6 293.5 all-reduce.5
  411.1 289.7 all-reduce.7
  746.1 289.8 all-reduce.9
  1039.1 40.0 reduce-scatter.16
  1082.4 41.1 reduce-scatter.14
  1250.4 32.5 reduce-scatter.18
  1286.1 34.2 reduce-scatter.20
  1323.4 34.0 reduce-scatter.22
  1360.6 34.0 reduce-scatter.12
  1397.0 154.9 all-reduce.11
where the time goes:
time: 1570 us; the launch traced here: 1560 us
  waiting for transfers between devices  1040 us (66%)
  matrix products  256 us (16%)
  other arithmetic  142 us (9%)
  local copies, waits for them, and re-layouts  53.8 us (3%)
  blocking collectives  49.1 us (3%)
  between operations  18.3 us (1%)
    psum x1, waiting for transfers between devices, shards(): attention_whole = lax.psum(attention_part, 'tensor')  293 us
    psum x1, waiting for transfers between devices, shards(): outer_rows = lax.psum(outer_part, 'tensor')  280 us
    psum x1, waiting for transfers between devices, shards(): normed_back = lax.psum(normed_part, 'tensor')  269 us
    psum x1, waiting for transfers between devices, shards(): lax.psum(input_part.astype(jnp.bfloat16), 'tensor').astype(jnp.float32)  156 us
    convert_element_type x4, other arithmetic, one_block(): score_grad = (probs * (prob_grad - centre)).astype(jnp.bfloat16)  42.8 us
    psum x1, blocking collectives, shards(): lax.psum((placed(jnp.sum(query_low.astype(jnp.float32), axis=0)), placed(...  40.3 us
    dot_general x4, matrix products, one_block(): jnp.einsum('qhd,khd->hqk', grad_block, values_split, preferred_element_ty...  39.8 us
    dot_general x6, matrix products, times_rows(): lax.dot_general(former, latter, (((1,), (1,)), ((), ())), preferred_eleme...  38.7 us
  transfers between devices with their start and end apart: 10, of which 6 were waited for; matrix products, arithmetic and copies ran while one was open for 18% of the time, Pallas kernels for 0%

commit v1 on v0

v1 whole, which is shorter than its diff:
```python
import math

import jax
import jax.numpy as jnp
from jax import lax
from jax.sharding import PartitionSpec as P

HD = 64


epsilon = 1e-05


def matmul(former, latter):
    return jnp.dot(former, latter, preferred_element_type=jnp.float32)


def times_rows(former, latter):
    return lax.dot_general(
        former, latter, (((1,), (1,)), ((), ())), preferred_element_type=jnp.float32
    )


def over_rows(former, latter):
    return lax.dot_general(
        former, latter, (((0,), (0,)), ((), ())), preferred_element_type=jnp.float32
    )


def layer_norm(hidden, norm_gain, norm_shift):
    centered = hidden - jnp.mean(hidden, axis=-1, keepdims=True)
    inverse = lax.rsqrt(jnp.mean(centered * centered, axis=-1, keepdims=True) + epsilon)
    normal = centered * inverse
    return (normal * norm_gain + norm_shift, normal, inverse)


def norm_back(upstream, normal, inverse, norm_gain):
    scaled = upstream * norm_gain
    return inverse * (
        scaled
        - jnp.mean(scaled, axis=-1, keepdims=True)
        - normal * jnp.mean(scaled * normal, axis=-1, keepdims=True)
    )


def gelu_parts(values):
    cumulative = 0.5 * (1.0 + jax.scipy.special.erf(values * 0.7071067811865476))
    slope = cumulative + values * jnp.exp(-0.5 * values * values) * 0.3989422804014327
    return (values * cumulative, slope)


def split_blocks(queries, keys_all, values_all):
    seq_len, local_width = queries.shape
    heads_here = local_width // HD
    block_rows = min(512, seq_len)
    block_count = seq_len // block_rows
    keys_split = keys_all.reshape(seq_len, heads_here, HD)
    values_split = values_all.reshape(seq_len, heads_here, HD)
    query_blocks = queries.reshape(block_count, block_rows, heads_here, HD)
    return (keys_split, values_split, query_blocks, block_count, block_rows, heads_here)


def block_scores(query_block, keys_split, key_valid, score_scale):
    scores = (
        jnp.einsum("qhd,khd->hqk", query_block, keys_split, preferred_element_type=jnp.float32)
        * score_scale
    )
    return jnp.where(key_valid[None, None, :], scores, -1e30)


def attend_forward(queries, keys_all, values_all, key_valid, score_scale):
    keys_split, values_split, query_blocks, block_count, block_rows, heads_here = split_blocks(
        queries, keys_all, values_all
    )

    def one_block(query_block):
        scores = block_scores(query_block, keys_split, key_valid, score_scale)
        row_peak = jnp.max(scores, axis=-1, keepdims=True)
        exponent = jnp.exp(scores - row_peak)
        row_total = jnp.sum(exponent, axis=-1, keepdims=True)
        probs = (exponent / row_total).astype(jnp.bfloat16)
        context = jnp.einsum(
            "hqk,khd->qhd", probs, values_split, preferred_element_type=jnp.float32
        )
        return (context, (row_peak + jnp.log(row_total))[..., 0])

    context, logsum = lax.map(one_block, query_blocks)
    return (context.reshape(queries.shape), logsum)


def attend_backward(queries, keys_all, values_all, key_valid, score_scale, logsum, context_grad):
    keys_split, values_split, query_blocks, block_count, block_rows, heads_here = split_blocks(
        queries, keys_all, values_all
    )
    grad_blocks = context_grad.reshape(block_count, block_rows, heads_here, HD)

    def one_block(carry, inputs):
        key_sum, value_sum = carry
        query_block, grad_block, logsum_block = inputs
        scores = block_scores(query_block, keys_split, key_valid, score_scale)
        probs = jnp.exp(scores - logsum_block[..., None])
        prob_grad = jnp.einsum(
            "qhd,khd->hqk", grad_block, values_split, preferred_element_type=jnp.float32
        )
        centre = jnp.sum(probs * prob_grad, axis=-1, keepdims=True)
        score_grad = (probs * (prob_grad - centre)).astype(jnp.bfloat16)
        query_grad = (
            jnp.einsum("hqk,khd->qhd", score_grad, keys_split, preferred_element_type=jnp.float32)
            * score_scale
        )
        key_sum = (
            key_sum
            + jnp.einsum(
                "hqk,qhd->khd", score_grad, query_block, preferred_element_type=jnp.float32
            )
            * score_scale
        )
        value_sum = value_sum + jnp.einsum(
            "hqk,qhd->khd",
            probs.astype(jnp.bfloat16),
            grad_block,
            preferred_element_type=jnp.float32,
        )
        return ((key_sum, value_sum), query_grad)

    zero_block = jnp.zeros(keys_split.shape, jnp.float32)
    (key_sum, value_sum), query_grads = lax.scan(
        one_block, (zero_block, zero_block), (query_blocks, grad_blocks, logsum)
    )
    return (
        query_grads.reshape(queries.shape),
        key_sum.reshape(queries.shape),
        value_sum.reshape(queries.shape),
    )


def flip(array_in, axis_name, bits):
    size = lax.axis_size(axis_name)
    return lax.ppermute(array_in, axis_name, [(i, i ^ bits) for i in range(size)])


def total(array_in, axis_names):
    for name in axis_names:
        bits = 1
        while bits < lax.axis_size(name):
            array_in = array_in + flip(array_in, name, bits)
            bits *= 2
    return array_in


def shards(
    hidden_in,
    lengths,
    query_weight,
    query_bias,
    key_weight,
    value_weight,
    value_bias,
    output_weight,
    output_bias,
    first_gain,
    first_shift,
    inner_weight,
    inner_bias,
    outer_weight,
    outer_bias,
    second_gain,
    second_shift,
    cotangent,
    teacher,
):
    seq_len, model_width = hidden_in.shape
    ranks = lax.axis_size("tensor")
    rank = lax.axis_index("tensor")
    copies = lax.axis_size("dp")
    copy = lax.axis_index("dp")
    share_rows = seq_len // ranks
    heads_width = query_weight.shape[1]
    units = inner_weight.shape[1]
    score_scale = 1.0 / math.sqrt(HD)
    row_valid = jnp.arange(seq_len, dtype=jnp.int32) < lengths[0]

    def take_own(array_in):
        return lax.dynamic_slice_in_dim(array_in, rank * share_rows, share_rows, 0)

    def gather(weight):
        rows = weight.shape[0] // copies
        part = lax.dynamic_slice_in_dim(weight, copy * rows, rows, 0)
        others = jnp.stack([flip(part, "tensor", s) for s in range(1, ranks)])
        others = lax.all_gather(others, "dp", axis=1, tiled=True)
        return [weight] + [others[s] for s in range(ranks - 1)]

    output_weights = gather(output_weight)
    inner_weights = gather(inner_weight)
    outer_weights = gather(outer_weight)
    inner_biases = [inner_bias] + [flip(inner_bias, "tensor", s) for s in range(1, ranks)]
    token_total = total(lengths, ("dp",))[0].astype(jnp.float32)
    grad_scale = seq_len * copies / (2.0 * token_total)

    def spread(array_in):
        own = []
        for s in range(ranks):
            start = (rank ^ s) * share_rows
            own.append(lax.dynamic_slice_in_dim(array_in, start, share_rows, 0))
        return own

    def exchange(blocks):
        return [blocks[0]] + [flip(blocks[s], "tensor", s) for s in range(1, ranks)]

    queries = (matmul(hidden_in, query_weight) + query_bias).astype(jnp.bfloat16)
    keys_all = matmul(hidden_in, key_weight).astype(jnp.bfloat16)
    values_all = (matmul(hidden_in, value_weight) + value_bias).astype(jnp.bfloat16)
    context, logsum = attend_forward(queries, keys_all, values_all, row_valid, score_scale)
    contexts = exchange(spread(context.astype(jnp.bfloat16)))

    hidden_own = take_own(hidden_in).astype(jnp.float32)
    attention = sum(times_rows(c, w) for c, w in zip(contexts, output_weights))
    normed, normal_one, inverse_one = layer_norm(
        hidden_own + (attention + output_bias), first_gain, first_shift
    )
    normed_low = normed.astype(jnp.bfloat16)
    activated, slopes = [], []
    branch = outer_bias.astype(jnp.float32)
    for s in range(ranks):
        value, slope = gelu_parts(matmul(normed_low, inner_weights[s]) + inner_biases[s])
        activated.append(value.astype(jnp.bfloat16))
        slopes.append(slope.astype(jnp.bfloat16))
        branch = branch + times_rows(activated[s], outer_weights[s])
    final, normal_two, inverse_two = layer_norm(normed + branch, second_gain, second_shift)
    row_mask = take_own(row_valid)[:, None]
    difference = final - take_own(teacher).astype(jnp.float32)
    loss_part = jnp.sum(jnp.where(row_mask, difference * difference, 0.0))
    final_grad = jnp.where(
        row_mask, take_own(cotangent).astype(jnp.float32) + grad_scale * difference, 0.0
    )
    second_grad = norm_back(final_grad, normal_two, inverse_two, second_gain)
    branch_low = second_grad.astype(jnp.bfloat16)
    inner_lows = []
    normed_grad = second_grad
    for s in range(ranks):
        inner_low = (matmul(branch_low, outer_weights[s]) * slopes[s]).astype(jnp.bfloat16)
        inner_lows.append(inner_low)
        normed_grad = normed_grad + times_rows(inner_low, inner_weights[s])
    first_grad = norm_back(normed_grad, normal_one, inverse_one, first_gain)
    attention_low = first_grad.astype(jnp.bfloat16)
    grads = exchange([matmul(attention_low, w).astype(jnp.bfloat16) for w in output_weights])
    context_grad = jnp.zeros((seq_len, heads_width), jnp.bfloat16)
    for s in range(ranks):
        context_grad = lax.dynamic_update_slice_in_dim(
            context_grad, grads[s], (rank ^ s) * share_rows, 0
        )

    def reduce(former, latter):
        whole = over_rows(former, latter).astype(jnp.bfloat16)
        rows = lax.psum_scatter(whole, "dp", scatter_dimension=0, tiled=True)
        return sum(g.astype(jnp.float32) for g in exchange(jnp.split(rows, ranks, axis=1)))

    activated_all = jnp.concatenate(activated, axis=1)
    inner_low_all = jnp.concatenate(inner_lows, axis=1)
    outer_weight_grad = reduce(branch_low, activated_all)
    inner_weight_grad = reduce(normed_low, inner_low_all)
    output_weight_grad = reduce(attention_low, jnp.concatenate(contexts, axis=1))

    query_grad, key_grad, value_grad = attend_backward(
        queries, keys_all, values_all, row_valid, score_scale, logsum, context_grad
    )
    query_low = query_grad.astype(jnp.bfloat16)
    key_low = key_grad.astype(jnp.bfloat16)
    value_low = value_grad.astype(jnp.bfloat16)
    input_part = (
        times_rows(query_low, query_weight)
        + times_rows(key_low, key_weight)
        + times_rows(value_low, value_weight)
    )
    input_rows = first_grad + lax.psum_scatter(
        input_part.astype(jnp.bfloat16), "tensor", scatter_dimension=0, tiled=True
    ).astype(jnp.float32)
    qkv_low = jnp.concatenate([query_low, key_low, value_low], axis=1)
    qkv_sum = lax.psum_scatter(
        over_rows(hidden_in, qkv_low).astype(jnp.bfloat16), "dp", scatter_dimension=0, tiled=True
    ).astype(jnp.float32)
    query_weight_grad, key_weight_grad, value_weight_grad = jnp.split(qkv_sum, 3, axis=1)

    def column_sums(array_in):
        return jnp.sum(array_in.astype(jnp.float32), axis=0)

    def placed(vector_in):
        zeros = jnp.zeros((vector_in.shape[0] * ranks,), jnp.float32)
        return lax.dynamic_update_slice_in_dim(zeros, vector_in, rank * vector_in.shape[0], 0)

    inner_sums = column_sums(inner_low_all).reshape(ranks, units)
    inner_sums = jnp.concatenate(
        [lax.dynamic_index_in_dim(inner_sums, rank ^ s, 0, keepdims=False) for s in range(ranks)]
    )
    vectors = [
        inner_sums,
        column_sums(attention_low),
        column_sums(normed_grad * normal_one),
        column_sums(normed_grad),
        column_sums(branch_low),
        column_sums(final_grad * normal_two),
        column_sums(final_grad),
        jnp.full((model_width,), loss_part),
    ]
    vectors = total(jnp.concatenate(vectors).reshape(-1, model_width), ("dp", "tensor"))
    late = jnp.stack([placed(column_sums(query_low)), placed(column_sums(value_low))])
    late = total(late, ("dp", "tensor"))
    wide = inner_sums.shape[0] // model_width
    inner_bias_grad = vectors[:wide].reshape(-1)
    (
        output_bias_grad,
        first_gain_grad,
        first_shift_grad,
        outer_bias_grad,
        second_gain_grad,
        second_shift_grad,
    ) = [vectors[wide + i] for i in range(6)]
    return (
        final.astype(jnp.bfloat16),
        vectors[wide + 6, 0] / token_total,
        input_rows,
        query_weight_grad,
        late[0],
        key_weight_grad,
        value_weight_grad,
        late[1],
        output_weight_grad,
        output_bias_grad,
        first_gain_grad,
        first_shift_grad,
        inner_weight_grad,
        inner_bias_grad,
        outer_weight_grad,
        outer_bias_grad,
        second_gain_grad,
        second_shift_grad,
    )


def solution(mesh):
    rows, columns, split = P("dp", None), P(None, "tensor"), P("dp", "tensor")
    part, whole, own = P("tensor"), P(), P(("dp", "tensor"), None)
    in_specs = (
        rows,
        P("dp"),
        columns,
        part,
        columns,
        columns,
        part,
        columns,
        whole,
        whole,
        whole,
        columns,
        part,
        columns,
        whole,
        whole,
        whole,
        rows,
        rows,
    )
    out_specs = (
        own,
        whole,
        own,
        split,
        whole,
        split,
        split,
        whole,
        split,
        whole,
        whole,
        whole,
        split,
        whole,
        split,
        whole,
        whole,
        whole,
    )
    return jax.shard_map(shards, mesh=mesh, in_specs=in_specs, out_specs=out_specs, check_vma=False)
```

time: 1570 us -> 833 us (0.53)
  waiting for transfers between devices: 1040 us -> 318 us
  starting transfers between devices: 1.26 us -> 70.6 us
  blocking collectives: 49.1 us -> 0 us
  other arithmetic: 142 us -> 92.9 us
    psum x4 -> x0, waiting for transfers between devices: 998 us -> none  [the longest x1 293 us: shards(): attention_whole = lax.psum(attention_part, 'tensor')]
    reduce_scatter x3 -> x4, waiting for transfers between devices: 35.5 us -> 236 us  [the longest x3 152 us: reduce(): rows = lax.psum_scatter(whole, 'dp', scatter_dimension=0, tiled=True)]
    ppermute x0 -> x40, waiting for transfers between devices: none -> 82.2 us  [flip(): lax.ppermute(array_in, axis_name, [(i, i ^ bits) for i in range(size)])]
    ppermute x0 -> x40, starting transfers between devices: none -> 70 us  [flip(): lax.ppermute(array_in, axis_name, [(i, i ^ bits) for i in range(size)])]
    psum x2 -> x0, blocking collectives: 49.1 us -> none  [the longest x1 40.3 us: shards(): lax.psum((placed(jnp.sum(query_low.astype(jnp.float32), axis=0)), placed(...]
    reduce_sum x10 -> x6, other arithmetic: 51.8 us -> 12.7 us  [column_sums(): return jnp.sum(array_in.astype(jnp.float32), axis=0)]
    dot_general x6 -> x4, matrix products: 34.7 us -> 26.9 us  [over_rows(): lax.dot_general(former, latter, (((0,), (0,)), ((), ())), preferred_eleme...]
    dot_general x6 -> x15, matrix products: 38.7 us -> 32.3 us  [times_rows(): lax.dot_general(former, latter, (((1,), (1,)), ((), ())), preferred_eleme...]
  transfers between devices with their start and end apart: 10 -> 48, of which waited for: 6 -> 25; matrix products, arithmetic and copies ran while one was open for 18% -> 19% of each run, Pallas kernels for 0% -> 0%
where the time goes in v1:
time: 833 us; the launch traced here: 822 us
  waiting for transfers between devices  318 us (38%)
  matrix products  268 us (32%)
  other arithmetic  92.9 us (11%)
  starting transfers between devices  70.6 us (8%)
  local copies, waits for them, and re-layouts  52.1 us (6%)
  between operations  20 us (2%)
    reduce_scatter x3, waiting for transfers between devices, reduce(): rows = lax.psum_scatter(whole, 'dp', scatter_dimension=0, tiled=True)  152 us
    reduce_scatter x1, waiting for transfers between devices, shards(): lax.psum_scatter(input_part.astype(jnp.bfloat16), 'tensor', scatter_dimen...  83.8 us
    ppermute x40, waiting for transfers between devices, flip(): lax.ppermute(array_in, axis_name, [(i, i ^ bits) for i in range(size)])  82.2 us
    ppermute x40, starting transfers between devices, flip(): lax.ppermute(array_in, axis_name, [(i, i ^ bits) for i in range(size)])  70 us
    dot_general x4, matrix products, one_block(): jnp.einsum('qhd,khd->hqk', grad_block, values_split, preferred_element_ty...  43.8 us
    convert_element_type x4, other arithmetic, one_block(): score_grad = (probs * (prob_grad - centre)).astype(jnp.bfloat16)  42.6 us
    dot_general x15, matrix products, matmul(): return jnp.dot(former, latter, preferred_element_type=jnp.float32)  36.7 us
    dot_general x15, matrix products, times_rows(): lax.dot_general(former, latter, (((1,), (1,)), ((), ())), preferred_eleme...  32.3 us
  transfers between devices with their start and end apart: 48, of which 25 were waited for; matrix products, arithmetic and copies ran while one was open for 19% of the time, Pallas kernels for 0%

profile of v1, /device:TPU:0, one launch (start us, length us, event | category | flops | bytes accessed | tf_op | source)
XLA Modules:
  0.0 822.0 jit_solution(8995926027960249381)
XLA Ops:
  24.4 15.4 %collective-permute-done.7 = bf16[128,1024]{1,0:T(8,128)(2,1)S(1)} collective-permute-done((bf16[128,1024]{1,0:T(8,128)(2,1)S(1)}, bf16[128,1024]{1,0:T(8,128)(2,1)S(1)}, u32[]{:S(2)}, u32[]{:S(2)}) %collective-permute-start.7) | collective-permute-done | bytes 262176 | tf_op jit(solution)/shard_map/ppermute | solution.py:139
  73.5 54.0 %while.28 = (s32[]{:T(128)}, bf16[4,512,4,64]{1,3,2,0:T(8,128)(2,1)}, f32[4,4,512]{2,1,0:T(4,128)S(1)}, bf16[4,512,4,64]{1,3,2,0:T(8,128)(2,1)}, bf16[2048,4,64]...) while((s32[]{:T(128)}, bf16[4,512,4,64]{1,3,2,0:T(8,128)(2,1)}, ...), condition=%wide.region_3.4_spmd.clone, body=%wide.region_0.3_spmd.clone.sunk | while | flops 1124073472 | bytes 57484408 | solution.py:87
  156.7 9.8 %collective-permute-done.4 = bf16[512,256]{0,1:T(8,128)(2,1)} collective-permute-done((bf16[512,256]{0,1:T(8,128)(2,1)}, bf16[512,256]{0,1:T(8,128)(2,1)}, u32[]{:S(2)}, u32[]{:S(2)}) %collective-permute-start.4) | collective-permute-done | bytes 262176 | tf_op jit(solution)/shard_map/ppermute | solution.py:139
  242.4 12.6 %collective-permute-done.24 = bf16[512,256]{1,0:T(8,128)(2,1)S(1)} collective-permute-done((bf16[512,256]{1,0:T(8,128)(2,1)}, bf16[512,256]{1,0:T(8,128)(2,1)S(1)}, u32[]{:S(2)}, u32[]{:S(2)}) %collective-permute-start.24) | collective-permute-done | bytes 262176 | tf_op jit(solution)/shard_map/ppermute | solution.py:139
  260.7 185.6 %while.29 = (s32[]{:T(128)}, f32[2048,4,64]{0,2,1:T(8,128)S(1)}, f32[2048,4,64]{0,2,1:T(8,128)}, bf16[4,512,4,64]{1,3,2,0:T(8,128)(2,1)}, bf16[4,512,4,64]{1,3,2...) while((s32[]{:T(128)}, f32[2048,4,64]{0,2,1:T(8,128)S(1)}, ...), condition=%wide.region_22.23_spmd.clone, body=%wide.region_20.22_spmd.clone.sunk | while | flops 2750021632 | bytes 281611008 | solution.py:127
  266.3 10.9 %multiply_reduce_fusion.10 = (f32[4,512]{1,0:T(4,128)S(1)}, f32[4,512,2048]{2,1,0:T(8,128)}) fusion(f32[4,512,2048]{2,1,0:T(8,128)S(1)} %fusion.216, f32[4,512]{1,0:T(4,128)S(1)} %dynamic-slice_bitcast_fusion.2, pred[2048]{0:T(1024)(128)(4,1)S(1)} %iota_compare_fusion.5, bf16[2048,4,64]{0,2,1:T(8,128)(2,1)} %get-tuple-element.540, ...), kind=kOutput, calls=%fused_computation.19.clone.1 | convolution fusion | flops 557840384 | bytes 34884096 | tf_op jit(solution)/shard_map/while/body/eval_jaxpr/qhd,khd->hqk/dot_general | solution.py:102
  277.2 10.7 %multiply_convert_fusion.10 = bf16[4,512,2048]{2,1,0:T(8,128)(2,1)} fusion(f32[4,512,2048]{2,1,0:T(8,128)} %get-tuple-element.482, f32[4,512,2048]{2,1,0:T(8,128)S(1)} %fusion.216, f32[4,512]{1,0:T(4,128)S(1)} %get-tuple-element.483, f32[4,512]{1,0:T(4,128)S(1)} %dynamic-slice_bitcast_fusion.2, pred[2048]{0:T(1024)(128)(4,1)S(1)} %iota_compare_fusion.5), kind=kLoop, calls=%fused_computation.18.clone.1 | loop fusion | flops 25165824 | bytes 41961472 | tf_op jit(solution)/shard_map/while/body/eval_jaxpr/convert_element_type | solution.py:106
  293.3 7.7 fusion.219
  312.3 10.9 %multiply_reduce_fusion.10 = (f32[4,512]{1,0:T(4,128)S(1)}, f32[4,512,2048]{2,1,0:T(8,128)}) fusion(f32[4,512,2048]{2,1,0:T(8,128)S(1)} %fusion.216, f32[4,512]{1,0:T(4,128)S(1)} %dynamic-slice_bitcast_fusion.2, pred[2048]{0:T(1024)(128)(4,1)S(1)} %iota_compare_fusion.5, bf16[2048,4,64]{0,2,1:T(8,128)(2,1)} %get-tuple-element.540, ...), kind=kOutput, calls=%fused_computation.19.clone.1 | convolution fusion | flops 557840384 | bytes 34884096 | tf_op jit(solution)/shard_map/while/body/eval_jaxpr/qhd,khd->hqk/dot_general | solution.py:102
  323.2 10.7 %multiply_convert_fusion.10 = bf16[4,512,2048]{2,1,0:T(8,128)(2,1)} fusion(f32[4,512,2048]{2,1,0:T(8,128)} %get-tuple-element.482, f32[4,512,2048]{2,1,0:T(8,128)S(1)} %fusion.216, f32[4,512]{1,0:T(4,128)S(1)} %get-tuple-element.483, f32[4,512]{1,0:T(4,128)S(1)} %dynamic-slice_bitcast_fusion.2, pred[2048]{0:T(1024)(128)(4,1)S(1)} %iota_compare_fusion.5), kind=kLoop, calls=%fused_computation.18.clone.1 | loop fusion | flops 25165824 | bytes 41961472 | tf_op jit(solution)/shard_map/while/body/eval_jaxpr/convert_element_type | solution.py:106
  339.3 7.7 fusion.219
  358.7 10.9 %multiply_reduce_fusion.10 = (f32[4,512]{1,0:T(4,128)S(1)}, f32[4,512,2048]{2,1,0:T(8,128)}) fusion(f32[4,512,2048]{2,1,0:T(8,128)S(1)} %fusion.216, f32[4,512]{1,0:T(4,128)S(1)} %dynamic-slice_bitcast_fusion.2, pred[2048]{0:T(1024)(128)(4,1)S(1)} %iota_compare_fusion.5, bf16[2048,4,64]{0,2,1:T(8,128)(2,1)} %get-tuple-element.540, ...), kind=kOutput, calls=%fused_computation.19.clone.1 | convolution fusion | flops 557840384 | bytes 34884096 | tf_op jit(solution)/shard_map/while/body/eval_jaxpr/qhd,khd->hqk/dot_general | solution.py:102
  369.6 10.7 %multiply_convert_fusion.10 = bf16[4,512,2048]{2,1,0:T(8,128)(2,1)} fusion(f32[4,512,2048]{2,1,0:T(8,128)} %get-tuple-element.482, f32[4,512,2048]{2,1,0:T(8,128)S(1)} %fusion.216, f32[4,512]{1,0:T(4,128)S(1)} %get-tuple-element.483, f32[4,512]{1,0:T(4,128)S(1)} %dynamic-slice_bitcast_fusion.2, pred[2048]{0:T(1024)(128)(4,1)S(1)} %iota_compare_fusion.5), kind=kLoop, calls=%fused_computation.18.clone.1 | loop fusion | flops 25165824 | bytes 41961472 | tf_op jit(solution)/shard_map/while/body/eval_jaxpr/convert_element_type | solution.py:106
  385.7 7.7 fusion.219
  405.1 10.9 %multiply_reduce_fusion.10 = (f32[4,512]{1,0:T(4,128)S(1)}, f32[4,512,2048]{2,1,0:T(8,128)}) fusion(f32[4,512,2048]{2,1,0:T(8,128)S(1)} %fusion.216, f32[4,512]{1,0:T(4,128)S(1)} %dynamic-slice_bitcast_fusion.2, pred[2048]{0:T(1024)(128)(4,1)S(1)} %iota_compare_fusion.5, bf16[2048,4,64]{0,2,1:T(8,128)(2,1)} %get-tuple-element.540, ...), kind=kOutput, calls=%fused_computation.19.clone.1 | convolution fusion | flops 557840384 | bytes 34884096 | tf_op jit(solution)/shard_map/while/body/eval_jaxpr/qhd,khd->hqk/dot_general | solution.py:102
  416.0 10.7 %multiply_convert_fusion.10 = bf16[4,512,2048]{2,1,0:T(8,128)(2,1)} fusion(f32[4,512,2048]{2,1,0:T(8,128)} %get-tuple-element.482, f32[4,512,2048]{2,1,0:T(8,128)S(1)} %fusion.216, f32[4,512]{1,0:T(4,128)S(1)} %get-tuple-element.483, f32[4,512]{1,0:T(4,128)S(1)} %dynamic-slice_bitcast_fusion.2, pred[2048]{0:T(1024)(128)(4,1)S(1)} %iota_compare_fusion.5), kind=kLoop, calls=%fused_computation.18.clone.1 | loop fusion | flops 25165824 | bytes 41961472 | tf_op jit(solution)/shard_map/while/body/eval_jaxpr/convert_element_type | solution.py:106
  432.1 7.7 fusion.219
  462.7 9.8 %convolution_convert_fusion = bf16[1024,4096]{1,0:T(8,128)(2,1)} fusion(bf16[512,1024]{1,0:T(8,128)(2,1)S(1)} %copy-done.23, bf16[512,1024]{1,0:T(8,128)(2,1)S(1)} %copy-done.64, bf16[512,1024]{1,0:T(8,128)(2,1)} %get-tuple-element.359, bf16[512,1024]{1,0:T(8,128)(2,1)} %get-tuple-element.361, bf16[512,1024]{1,0:T(8,128)(2,1)} %copy-done.66), kind=kOutput, calls=%fused_computation.52 | convolution fusion | flops 4315938816 | bytes 13631488 | tf_op jit(solution)/shard_map/dot_general | solution.py:25
  482.5 9.7 %convolution_convert_fusion.1 = bf16[1024,4096]{1,0:T(8,128)(2,1)} fusion(bf16[512,1024]{1,0:T(8,128)(2,1)S(1)} %copy-done.29, bf16[512,1024]{1,0:T(8,128)(2,1)S(1)} %copy-done.17, bf16[512,1024]{1,0:T(8,128)(2,1)} %copy-done.33, bf16[512,1024]{1,0:T(8,128)(2,1)} %copy-done.32, bf16[512,1024]{1,0:T(8,128)(2,1)} %copy-done.30), kind=kOutput, calls=%fused_computation.53 | convolution fusion | flops 4315938816 | bytes 13631488 | tf_op jit(solution)/shard_map/dot_general | solution.py:25
  529.3 12.8 %reduce-scatter.10.cloned.1.call-done = bf16[128,1024]{1,0:T(8,128)(2,1)} async-done(((bf16[1024,1024]{1,0:T(8,128)(2,1)}), bf16[128,1024]{1,0:T(8,128)(2,1)}) %reduce-scatter.10.cloned.1.call-update) | async-done | bytes 262160 | tf_op jit(solution)/shard_map/reduce_scatter | solution.py:255
  554.6 62.3 %reduce-scatter.14.cloned.1.call-done = bf16[128,4096]{1,0:T(8,128)(2,1)} async-done(((bf16[1024,4096]{1,0:T(8,128)(2,1)}), bf16[128,4096]{1,0:T(8,128)(2,1)}) %reduce-scatter.14.cloned.1.call-update) | async-done | bytes 1048592 | tf_op jit(solution)/shard_map/reduce_scatter | solution.py:255
  623.2 83.8 %reduce-scatter.8.cloned.1.call-done = bf16[512,1024]{1,0:T(8,128)(2,1)} async-done(((bf16[2048,1024]{1,0:T(8,128)(2,1)}), bf16[512,1024]{1,0:T(8,128)(2,1)}) %reduce-scatter.8.cloned.1.call-update) | async-done | bytes 1048592 | tf_op jit(solution)/shard_map/reduce_scatter | solution.py:275
  710.7 76.9 %reduce-scatter.12.cloned.1.call-done = bf16[128,4096]{1,0:T(8,128)(2,1)} async-done(((bf16[1024,4096]{1,0:T(8,128)(2,1)}), bf16[128,4096]{1,0:T(8,128)(2,1)}) %reduce-scatter.12.cloned.1.call-update) | async-done | bytes 1048592 | tf_op jit(solution)/shard_map/reduce_scatter | solution.py:255
  801.5 10.2 %collective-permute-done.35 = bf16[128,1024]{1,0:T(8,128)(2,1)S(1)} collective-permute-done((bf16[128,1024]{1,0:T(8,128)(2,1)S(1)}, bf16[128,1024]{1,0:T(8,128)(2,1)S(1)}, u32[]{:S(2)}, u32[]{:S(2)}) %collective-permute-start.35) | collective-permute-done | bytes 262176 | tf_op jit(solution)/shard_map/ppermute | solution.py:139
  (456 shorter events, 380.5 us)
Async XLA Ops:
  7.2 147.8 %all-gather.4.cloned.1.call-start = ((), (), s32[]{:S(2)}) async-start(), calls=%async_computation.5 | async-start | bytes 1769472 | tf_op jit(solution)/shard_map/all_gather | solution.py:190
  20.7 157.2 %all-gather.6.cloned.1.call-start = ((), (), s32[]{:S(2)}) async-start(), calls=%async_computation.6 | async-start | bytes 7077888 | tf_op jit(solution)/shard_map/all_gather | solution.py:190
  20.8 18.9 %collective-permute-start.7 = (bf16[128,1024]{1,0:T(8,128)(2,1)S(1)}, bf16[128,1024]{1,0:T(8,128)(2,1)S(1)}, u32[]{:S(2)}, u32[]{:S(2)}) collective-permute-start(bf16[128,1024]{1,0:T(8,128)(2,1)S(1)} %constant_dynamic-slice_fusion.5), channel_id=1, source_target_pairs={{0,2},{1,3},{2,0},{3,1},{4,6},{5,7},{6,4},{7,5},{8,10},{9,11},{10,... | collective-permute-start | bytes 786440 | tf_op jit(solution)/shard_map/ppermute | solution.py:139
  41.8 145.8 %all-gather.8.cloned.1.call-start = ((), (), s32[]{:S(2)}) async-start(), calls=%async_computation.7 | async-start | bytes 7077888 | tf_op jit(solution)/shard_map/all_gather | solution.py:190
  42.9 24.9 %collective-permute-start.10 = (bf16[128,1024]{1,0:T(8,128)(2,1)S(1)}, bf16[128,1024]{1,0:T(8,128)(2,1)}, u32[]{:S(2)}, u32[]{:S(2)}) collective-permute-start(bf16[128,1024]{1,0:T(8,128)(2,1)S(1)} %constant_dynamic-slice_fusion.4), channel_id=1, source_target_pairs={{0,1},{1,0},{2,3},{3,2},{4,5},{5,4},{6,7},{7,6},{8,9},{9,8},{10,11... | collective-permute-start | bytes 786440 | tf_op jit(solution)/shard_map/ppermute | solution.py:139
  47.8 22.4 %collective-permute-start.11 = (bf16[128,1024]{1,0:T(8,128)(2,1)S(1)}, bf16[128,1024]{1,0:T(8,128)(2,1)}, u32[]{:S(2)}, u32[]{:S(2)}) collective-permute-start(bf16[128,1024]{1,0:T(8,128)(2,1)S(1)} %constant_dynamic-slice_fusion.4), channel_id=1, source_target_pairs={{0,2},{1,3},{2,0},{3,1},{4,6},{5,7},{6,4},{7,5},{8,10},{9,11},{10,... | collective-permute-start | bytes 786440 | tf_op jit(solution)/shard_map/ppermute | solution.py:139
  47.8 22.4 %collective-permute-start.12 = (bf16[128,1024]{1,0:T(8,128)(2,1)S(1)}, bf16[128,1024]{1,0:T(8,128)(2,1)}, u32[]{:S(2)}, u32[]{:S(2)}) collective-permute-start(bf16[128,1024]{1,0:T(8,128)(2,1)S(1)} %constant_dynamic-slice_fusion.4), channel_id=1, source_target_pairs={{0,3},{1,2},{2,1},{3,0},{4,7},{5,6},{6,5},{7,4},{8,11},{9,10},{10,... | collective-permute-start | bytes 786440 | tf_op jit(solution)/shard_map/ppermute | solution.py:139
  50.2 99.6 %collective-permute-start.9 = (bf16[1024]{0:T(1024)(128)(2,1)}, bf16[1024]{0:T(1024)(128)(2,1)}, u32[]{:S(2)}, u32[]{:S(2)}) collective-permute-start(bf16[1024]{0:T(1024)(128)(2,1)} %param.35), channel_id=1, source_target_pairs={{0,1},{1,0},{2,3},{3,2},{4,5},{5,4},{6,7},{7,6},{8,9},{9,8},{10,11... | collective-permute-start | bytes 6152 | tf_op jit(solution)/shard_map/ppermute | solution.py:139
  51.3 102.4 %collective-permute-start.13 = (bf16[1024]{0:T(1024)(128)(2,1)}, bf16[1024]{0:T(1024)(128)(2,1)}, u32[]{:S(2)}, u32[]{:S(2)}) collective-permute-start(bf16[1024]{0:T(1024)(128)(2,1)} %param.35), channel_id=1, source_target_pairs={{0,2},{1,3},{2,0},{3,1},{4,6},{5,7},{6,4},{7,5},{8,10},{9,11},{10,... | collective-permute-start | bytes 6152 | tf_op jit(solution)/shard_map/ppermute | solution.py:139
  67.7 86.6 %collective-permute-start.14 = (bf16[1024]{0:T(1024)(128)(2,1)}, bf16[1024]{0:T(1024)(128)(2,1)}, u32[]{:S(2)}, u32[]{:S(2)}) collective-permute-start(bf16[1024]{0:T(1024)(128)(2,1)} %param.35), channel_id=1, source_target_pairs={{0,3},{1,2},{2,1},{3,0},{4,7},{5,6},{6,5},{7,4},{8,11},{9,10},{10,... | collective-permute-start | bytes 6152 | tf_op jit(solution)/shard_map/ppermute | solution.py:139
  70.2 70.4 %collective-permute-start.15 = (s32[1]{0:T(128)}, s32[1]{0:T(128)}, u32[]{:S(2)}, u32[]{:S(2)}) collective-permute-start(s32[1]{0:T(128)} %param.24), channel_id=1, source_target_pairs={{0,4},{4,0},{8,12},{12,8},{16,20},{20,16},{24,28},{28,24},{1,5},{5... | collective-permute-start | bytes 20 | tf_op jit(solution)/shard_map/ppermute | solution.py:139
  72.3 455.8 %reduce-scatter.16.cloned.1.call-start = ((), (), s32[]{:S(2)}) async-start(), calls=%async_computation.12 | async-start | bytes 1769472
  133.1 21.9 %collective-permute-start = (bf16[512,256]{0,1:T(8,128)(2,1)}, bf16[512,256]{0,1:T(8,128)(2,1)}, u32[]{:S(2)}, u32[]{:S(2)}) collective-permute-start(bf16[512,256]{0,1:T(8,128)(2,1)} %get-tuple-element.337), channel_id=1, source_target_pairs={{0,1},{1,0},{2,3},{3,2},{4,5},{5,4},{6,7},{7,6},{8,9},{9,8},{10,11... | collective-permute-start | bytes 786440 | tf_op jit(solution)/shard_map/ppermute | solution.py:139
  234.0 21.0 %collective-permute-start.24 = (bf16[512,256]{1,0:T(8,128)(2,1)}, bf16[512,256]{1,0:T(8,128)(2,1)S(1)}, u32[]{:S(2)}, u32[]{:S(2)}) collective-permute-start(bf16[512,256]{1,0:T(8,128)(2,1)} %convolution_convert_fusion.5), channel_id=1, source_target_pairs={{0,2},{1,3},{2,0},{3,1},{4,6},{5,7},{6,4},{7,5},{8,10},{9,11},{10,... | collective-permute-start | bytes 786440 | tf_op jit(solution)/shard_map/ppermute | solution.py:139
  235.1 20.1 %collective-permute-start.25 = (bf16[512,256]{1,0:T(8,128)(2,1)}, bf16[512,256]{1,0:T(8,128)(2,1)S(1)}, u32[]{:S(2)}, u32[]{:S(2)}) collective-permute-start(bf16[512,256]{1,0:T(8,128)(2,1)} %convolution_convert_fusion.4), channel_id=1, source_target_pairs={{0,3},{1,2},{2,1},{3,0},{4,7},{5,6},{6,5},{7,4},{8,11},{9,10},{10,... | collective-permute-start | bytes 786440 | tf_op jit(solution)/shard_map/ppermute | solution.py:139
  457.1 85.0 %reduce-scatter.10.cloned.1.call-start = ((), (), s32[]{:S(2)}) async-start(), calls=%async_computation.9 | async-start | bytes 2359296 | tf_op jit(solution)/shard_map/reduce_scatter | solution.py:255
  461.2 155.7 %reduce-scatter.14.cloned.1.call-start = ((), (), s32[]{:S(2)}) async-start(), calls=%async_computation.11 | async-start | bytes 9437184 | tf_op jit(solution)/shard_map/reduce_scatter | solution.py:255
  472.5 234.4 %reduce-scatter.8.cloned.1.call-start = ((), (), s32[]{:S(2)}) async-start(), calls=%async_computation.8 | async-start | bytes 5242880 | tf_op jit(solution)/shard_map/reduce_scatter | solution.py:275
  481.0 306.6 %reduce-scatter.12.cloned.1.call-start = ((), (), s32[]{:S(2)}) async-start(), calls=%async_computation.10 | async-start | bytes 9437184 | tf_op jit(solution)/shard_map/reduce_scatter | solution.py:255
  618.8 174.0 %collective-permute-start.37 = (bf16[128,1024]{1,0:T(8,128)(2,1)}, bf16[128,1024]{1,0:T(8,128)(2,1)S(1)}, u32[]{:S(2)}, u32[]{:S(2)}) collective-permute-start(bf16[128,1024]{1,0:T(8,128)(2,1)} %get-tuple-element.329), channel_id=1, source_target_pairs={{0,1},{1,0},{2,3},{3,2},{4,5},{5,4},{6,7},{7,6},{8,9},{9,8},{10,11... | collective-permute-start | bytes 786440 | tf_op jit(solution)/shard_map/ppermute | solution.py:139
  620.3 173.0 %collective-permute-start.38 = (bf16[128,1024]{1,0:T(8,128)(2,1)S(1)}, bf16[128,1024]{1,0:T(8,128)(2,1)S(1)}, u32[]{:S(2)}, u32[]{:S(2)}) collective-permute-start(bf16[128,1024]{1,0:T(8,128)(2,1)S(1)} %get-tuple-element.331), channel_id=1, source_target_pairs={{0,2},{1,3},{2,0},{3,1},{4,6},{5,7},{6,4},{7,5},{8,10},{9,11},{10,... | collective-permute-start | bytes 786440 | tf_op jit(solution)/shard_map/ppermute | solution.py:139
  622.7 170.6 %collective-permute-start.39 = (bf16[128,1024]{1,0:T(8,128)(2,1)S(1)}, bf16[128,1024]{1,0:T(8,128)(2,1)S(1)}, u32[]{:S(2)}, u32[]{:S(2)}) collective-permute-start(bf16[128,1024]{1,0:T(8,128)(2,1)S(1)} %get-tuple-element.330), channel_id=1, source_target_pairs={{0,3},{1,2},{2,1},{3,0},{4,7},{5,6},{6,5},{7,4},{8,11},{9,10},{10,... | collective-permute-start | bytes 786440 | tf_op jit(solution)/shard_map/ppermute | solution.py:139
  790.4 21.3 %collective-permute-start.35 = (bf16[128,1024]{1,0:T(8,128)(2,1)S(1)}, bf16[128,1024]{1,0:T(8,128)(2,1)S(1)}, u32[]{:S(2)}, u32[]{:S(2)}) collective-permute-start(bf16[128,1024]{1,0:T(8,128)(2,1)S(1)} %get-tuple-element.334), channel_id=1, source_target_pairs={{0,2},{1,3},{2,0},{3,1},{4,6},{5,7},{6,4},{7,5},{8,10},{9,11},{10,... | collective-permute-start | bytes 786440 | tf_op jit(solution)/shard_map/ppermute | solution.py:139
  792.8 18.9 %collective-permute-start.36 = (bf16[128,1024]{1,0:T(8,128)(2,1)S(1)}, bf16[128,1024]{1,0:T(8,128)(2,1)S(1)}, u32[]{:S(2)}, u32[]{:S(2)}) collective-permute-start(bf16[128,1024]{1,0:T(8,128)(2,1)S(1)} %get-tuple-element.333), channel_id=1, source_target_pairs={{0,3},{1,2},{2,1},{3,0},{4,7},{5,6},{6,5},{7,4},{8,11},{9,10},{10,... | collective-permute-start | bytes 786440 | tf_op jit(solution)/shard_map/ppermute | solution.py:139
  (113 other events, 739.4 us)
Sparse Core Ops, SparseCore 0:
  20.8 24.9 all-gather.3
  47.8 45.3 all-gather.5
  95.1 45.3 all-gather.7
  457.2 40.5 reduce-scatter.15
  500.9 41.1 reduce-scatter.9
  545.4 71.4 reduce-scatter.13
  619.2 87.7 reduce-scatter.7
  710.4 77.1 reduce-scatter.11

commit v2 on v1

v2 whole, which is shorter than its diff:
```python
import jax
import jax.numpy as jnp
from jax import lax
from jax.experimental import pallas as pl
from jax.experimental.pallas import tpu as pltpu
from jax.sharding import PartitionSpec as P

HD = 64
PAIR = 128
VMEM_BYTES = 60000 * 1024


epsilon = 1e-05


def matmul(former, latter):
    return jnp.dot(former, latter, preferred_element_type=jnp.float32)


def times_rows(former, latter):
    return lax.dot_general(
        former, latter, (((1,), (1,)), ((), ())), preferred_element_type=jnp.float32
    )


def over_rows(former, latter):
    return lax.dot_general(
        former, latter, (((0,), (0,)), ((), ())), preferred_element_type=jnp.float32
    )


def layer_norm(hidden, norm_gain, norm_shift):
    centered = hidden - jnp.mean(hidden, axis=-1, keepdims=True)
    inverse = lax.rsqrt(jnp.mean(centered * centered, axis=-1, keepdims=True) + epsilon)
    normal = centered * inverse
    return (normal * norm_gain + norm_shift, normal, inverse)


def norm_back(upstream, normal, inverse, norm_gain):
    scaled = upstream * norm_gain
    return inverse * (
        scaled
        - jnp.mean(scaled, axis=-1, keepdims=True)
        - normal * jnp.mean(scaled * normal, axis=-1, keepdims=True)
    )


def gelu_parts(values):
    cumulative = 0.5 * (1.0 + jax.scipy.special.erf(values * 0.7071067811865476))
    slope = cumulative + values * jnp.exp(-0.5 * values * values) * 0.3989422804014327
    return (values * cumulative, slope)


def lanes(rows):
    return lax.broadcasted_iota(jnp.int32, (rows, PAIR), 1)


def in_head(lane, head):
    return (lane < HD) if head == 0 else (lane >= HD)


def extend(base, lane, head, first, offset):
    start = HD * (1 - head)
    high = offset.astype(jnp.bfloat16).astype(jnp.float32)
    middle = (offset - high).astype(jnp.bfloat16).astype(jnp.float32)
    out = jnp.where(lane == start, first, 0.0)
    out = jnp.where(lane == start + 1, -high, out)
    out = jnp.where(lane == start + 2, -middle, out)
    out = jnp.where(lane == start + 3, high + middle - offset, out)
    return jnp.where(in_head(lane, head), base, out).astype(jnp.bfloat16)


def extend_keys(keys, lane, head, row_start, length):
    start = HD * (1 - head)
    position = row_start + lax.broadcasted_iota(jnp.int32, keys.shape, 0)
    bias = jnp.where(position < length, 0.0, -1e30)
    ones = jnp.where((lane > start) & (lane < start + 4), 1.0, 0.0)
    side = jnp.where(lane == start, bias, ones)
    return jnp.where(in_head(lane, head), keys, side).astype(jnp.bfloat16)


def extend_values(values, lane, head):
    return jnp.where(in_head(lane, head), values, 1.0).astype(jnp.bfloat16)


def forward_kernel(length_ref, q_ref, k_ref, v_ref, context_ref, extended_ref, keys, values):
    @pl.when(pl.program_id(0) == 0)
    def _():
        lane = lanes(k_ref.shape[0])
        k_float = k_ref[...].astype(jnp.float32)
        v_float = v_ref[...].astype(jnp.float32)
        for head in range(2):
            keys[head] = extend_keys(k_float, lane, head, 0, length_ref[0])
            values[head] = extend_values(v_float, lane, head)

    lane = lanes(q_ref.shape[0])
    scaled = q_ref[...].astype(jnp.float32) * HD**-0.5
    contexts = []
    for head in range(2):
        plain = jnp.where(lane == HD * (1 - head), 1.0, 0.0)
        query = jnp.where(in_head(lane, head), scaled, plain).astype(jnp.bfloat16)
        scores = times_rows(query, keys[head])
        peak = jnp.max(scores, axis=1, keepdims=True)
        exponent = jnp.exp(scores - peak).astype(jnp.bfloat16)
        out = matmul(exponent, values[head])
        contexts.append(out / pltpu.roll(out, HD, 1))
        extended_ref[head] = extend(scaled, lane, head, 1.0, peak + jnp.log(out))
    context_ref[...] = jnp.where(lane < HD, contexts[0], contexts[1]).astype(jnp.bfloat16)


def attend_forward(length, qkv, pair):
    seq_len = qkv.shape[0]
    rows = min(256, seq_len)
    return pl.pallas_call(
        forward_kernel,
        grid_spec=pltpu.PrefetchScalarGridSpec(
            num_scalar_prefetch=1,
            grid=(seq_len // rows,),
            in_specs=[
                pl.BlockSpec((rows, PAIR), lambda i, n: (i, 3 * pair)),
                pl.BlockSpec((seq_len, PAIR), lambda i, n: (0, 3 * pair + 1)),
                pl.BlockSpec((seq_len, PAIR), lambda i, n: (0, 3 * pair + 2)),
            ],
            out_specs=[
                pl.BlockSpec((rows, PAIR), lambda i, n: (i, 0)),
                pl.BlockSpec((2, rows, PAIR), lambda i, n: (0, i, 0)),
            ],
            scratch_shapes=[pltpu.VMEM((2, seq_len, PAIR), jnp.bfloat16)] * 2,
        ),
        out_shape=[
            jax.ShapeDtypeStruct((seq_len, PAIR), jnp.bfloat16),
            jax.ShapeDtypeStruct((2, seq_len, PAIR), jnp.bfloat16),
        ],
        compiler_params=pltpu.CompilerParams(vmem_limit_bytes=VMEM_BYTES),
        cost_estimate=pl.CostEstimate(
            flops=8 * seq_len * seq_len * 2 * PAIR,
            bytes_accessed=12 * seq_len * PAIR,
            transcendentals=2 * seq_len * seq_len,
        ),
        name="attend_forward",
    )(length, qkv, qkv, qkv)


def backward_kernel(length_ref, extended_ref, k_ref, v_ref, context_ref, grad_ref, out_ref, grads, turned):
    step = pl.program_id(0)
    seq_len, rows = grad_ref.shape[0], k_ref.shape[0]

    @pl.when(step == 0)
    def _():
        def prepare(j, carry):
            here = pl.ds(pl.multiple_of(j * rows, rows), rows)
            lane = lanes(rows)
            grad = grad_ref[here, :].astype(jnp.float32)
            product = grad * context_ref[here, :].astype(jnp.float32)
            for head in range(2):
                centre = jnp.sum(
                    jnp.where(in_head(lane, head), product, 0.0), axis=1, keepdims=True
                )
                grads[head, here, :] = extend(grad, lane, head, 0.0, centre)
            return carry

        lax.fori_loop(0, seq_len // rows, prepare, 0)

    lane = lanes(rows)
    k_float = k_ref[...].astype(jnp.float32)
    v_float = v_ref[...].astype(jnp.float32)
    across = k_float.T.astype(jnp.bfloat16)
    key_grads, value_grads = [], []
    for head in range(2):
        keys = extend_keys(k_float, lane, head, step * rows, length_ref[0])
        values = extend_values(v_float, lane, head)
        query, grad = extended_ref[head], grads[head]
        probs = jnp.exp(times_rows(keys, query))
        score_grad = (probs * times_rows(values, grad)).astype(jnp.bfloat16)
        value_grads.append(matmul(probs.astype(jnp.bfloat16), grad))
        key_grads.append(matmul(score_grad, query))
        own = slice(HD * head, HD * (head + 1))
        part = matmul(across[own], score_grad)

        @pl.when(step == 0)
        def _():
            turned[own, :] = part

        @pl.when(step > 0)
        def _():
            turned[own, :] += part

    here = pl.ds(pl.multiple_of(step * rows, rows), rows)
    key_grad = jnp.where(lane < HD, key_grads[0], key_grads[1])
    value_grad = jnp.where(lane < HD, value_grads[0], value_grads[1])
    out_ref[here, PAIR : 2 * PAIR] = key_grad.astype(jnp.bfloat16)
    out_ref[here, 2 * PAIR :] = value_grad.astype(jnp.bfloat16)

    @pl.when(step == pl.num_programs(0) - 1)
    def _():
        def finish(j, carry):
            here = pl.ds(pl.multiple_of(j * rows, rows), rows)
            out_ref[here, :PAIR] = (turned[:, here].T * HD**-0.5).astype(jnp.bfloat16)
            return carry

        lax.fori_loop(0, seq_len // rows, finish, 0)


def attend_backward(length, extended, qkv, context, context_grad, pair):
    seq_len = qkv.shape[0]
    rows = min(256, seq_len)
    return pl.pallas_call(
        backward_kernel,
        grid_spec=pltpu.PrefetchScalarGridSpec(
            num_scalar_prefetch=1,
            grid=(seq_len // rows,),
            in_specs=[
                pl.BlockSpec((2, seq_len, PAIR), lambda i, n: (0, 0, 0)),
                pl.BlockSpec((rows, PAIR), lambda i, n: (i, 3 * pair + 1)),
                pl.BlockSpec((rows, PAIR), lambda i, n: (i, 3 * pair + 2)),
                pl.BlockSpec((seq_len, PAIR), lambda i, n: (0, 0)),
                pl.BlockSpec((seq_len, PAIR), lambda i, n: (0, pair)),
            ],
            out_specs=pl.BlockSpec((seq_len, 3 * PAIR), lambda i, n: (0, 0)),
            scratch_shapes=[
                pltpu.VMEM((2, seq_len, PAIR), jnp.bfloat16),
                pltpu.VMEM((PAIR, seq_len), jnp.float32),
            ],
        ),
        out_shape=jax.ShapeDtypeStruct((seq_len, 3 * PAIR), jnp.bfloat16),
        compiler_params=pltpu.CompilerParams(vmem_limit_bytes=VMEM_BYTES),
        cost_estimate=pl.CostEstimate(
            flops=20 * seq_len * seq_len * 2 * PAIR,
            bytes_accessed=20 * seq_len * PAIR,
            transcendentals=2 * seq_len * seq_len,
        ),
        name="attend_backward",
    )(length, extended, qkv, qkv, context, context_grad)


def flip(array_in, axis_name, bits):
    size = lax.axis_size(axis_name)
    return lax.ppermute(array_in, axis_name, [(i, i ^ bits) for i in range(size)])


def total(array_in, axis_names):
    for name in axis_names:
        bits = 1
        while bits < lax.axis_size(name):
            array_in = array_in + flip(array_in, name, bits)
            bits *= 2
    return array_in


def shards(
    hidden_in,
    lengths,
    query_weight,
    query_bias,
    key_weight,
    value_weight,
    value_bias,
    output_weight,
    output_bias,
    first_gain,
    first_shift,
    inner_weight,
    inner_bias,
    outer_weight,
    outer_bias,
    second_gain,
    second_shift,
    cotangent,
    teacher,
):
    seq_len, model_width = hidden_in.shape
    ranks = lax.axis_size("tensor")
    rank = lax.axis_index("tensor")
    copies = lax.axis_size("dp")
    copy = lax.axis_index("dp")
    share_rows = seq_len // ranks
    heads_width = query_weight.shape[1]
    units = inner_weight.shape[1]
    pairs = heads_width // PAIR
    row_valid = jnp.arange(seq_len, dtype=jnp.int32) < lengths[0]

    def take_own(array_in):
        return lax.dynamic_slice_in_dim(array_in, rank * share_rows, share_rows, 0)

    def by_pairs(*arrays):
        return jnp.concatenate(
            [a[..., p * PAIR : (p + 1) * PAIR] for p in range(pairs) for a in arrays], axis=-1
        )

    qkv_weight = by_pairs(query_weight, key_weight, value_weight)
    qkv_bias = by_pairs(query_bias, jnp.zeros_like(query_bias), value_bias)

    def gather(weight):
        rows = weight.shape[0] // copies
        part = lax.dynamic_slice_in_dim(weight, copy * rows, rows, 0)
        others = jnp.stack([flip(part, "tensor", s) for s in range(1, ranks)])
        others = lax.all_gather(others, "dp", axis=1, tiled=True)
        return [weight] + [others[s] for s in range(ranks - 1)]

    def spread(array_in):
        own = []
        for s in range(ranks):
            start = (rank ^ s) * share_rows
            own.append(lax.dynamic_slice_in_dim(array_in, start, share_rows, 0))
        return own

    def exchange(blocks):
        return [blocks[0]] + [flip(blocks[s], "tensor", s) for s in range(1, ranks)]

    def ordered(vector_in):
        table = vector_in.reshape(ranks, -1)
        return jnp.concatenate(
            [lax.dynamic_index_in_dim(table, rank ^ s, 0, keepdims=False) for s in range(ranks)]
        )

    early = gather(jnp.concatenate([inner_weight, output_weight], axis=1))
    inner_weights = [w[:, :units] for w in early]
    output_weight_all = jnp.concatenate([w[:, units:] for w in early], axis=1)
    outer_weights = gather(outer_weight)
    qkv_weights = gather(qkv_weight)
    inner_biases = [inner_bias] + [flip(inner_bias, "tensor", s) for s in range(1, ranks)]
    token_total = total(lengths, ("dp",))[0].astype(jnp.float32)
    grad_scale = seq_len * copies / (2.0 * token_total)

    qkv = (matmul(hidden_in, qkv_weight) + qkv_bias).astype(jnp.bfloat16)
    contexts, extended, received = [], [], []
    for pair in range(pairs):
        context, queries = attend_forward(lengths, qkv, pair)
        contexts.append(context)
        extended.append(queries)
        received.append(exchange(spread(context)))
    context_all = jnp.concatenate([received[p][s] for s in range(ranks) for p in range(pairs)], axis=1)

    hidden_own = take_own(hidden_in).astype(jnp.float32)
    attention = times_rows(context_all, output_weight_all)
    normed, normal_one, inverse_one = layer_norm(
        hidden_own + (attention + output_bias), first_gain, first_shift
    )
    normed_low = normed.astype(jnp.bfloat16)
    activated, slopes = [], []
    branch = outer_bias.astype(jnp.float32)
    for s in range(ranks):
        value, slope = gelu_parts(matmul(normed_low, inner_weights[s]) + inner_biases[s])
        activated.append(value.astype(jnp.bfloat16))
        slopes.append(slope.astype(jnp.bfloat16))
        branch = branch + times_rows(activated[s], outer_weights[s])
    final, normal_two, inverse_two = layer_norm(normed + branch, second_gain, second_shift)
    row_mask = take_own(row_valid)[:, None]
    difference = final - take_own(teacher).astype(jnp.float32)
    loss_part = jnp.sum(jnp.where(row_mask, difference * difference, 0.0))
    final_grad = jnp.where(
        row_mask, take_own(cotangent).astype(jnp.float32) + grad_scale * difference, 0.0
    )
    second_grad = norm_back(final_grad, normal_two, inverse_two, second_gain)
    branch_low = second_grad.astype(jnp.bfloat16)
    outer_whole = over_rows(branch_low, jnp.concatenate(activated, axis=1)).astype(jnp.bfloat16)
    inner_lows = []
    normed_grad = second_grad
    for s in range(ranks):
        inner_low = (matmul(branch_low, outer_weights[s]) * slopes[s]).astype(jnp.bfloat16)
        inner_lows.append(inner_low)
        normed_grad = normed_grad + times_rows(inner_low, inner_weights[s])
    first_grad = norm_back(normed_grad, normal_one, inverse_one, first_gain)
    attention_low = first_grad.astype(jnp.bfloat16)
    grad_all = matmul(attention_low, output_weight_all).astype(jnp.bfloat16)
    grads = exchange(jnp.split(grad_all, ranks, axis=1))
    context_grad = jnp.zeros((seq_len, heads_width), jnp.bfloat16)
    for s in range(ranks):
        context_grad = lax.dynamic_update_slice_in_dim(
            context_grad, grads[s], (rank ^ s) * share_rows, 0
        )

    inner_low_all = jnp.concatenate(inner_lows, axis=1)
    inner_whole = over_rows(normed_low, inner_low_all).astype(jnp.bfloat16)
    output_whole = over_rows(attention_low, context_all).astype(jnp.bfloat16)

    def reduce_copies(whole):
        rows = whole.shape[0] // copies
        bits = [1]
        while 2 * bits[0] < copies:
            bits.insert(0, 2 * bits[0])
        bits = [1] + bits[:-1]
        blocks = whole.reshape(copies, rows, -1)
        left = list(range(copies.bit_length() - 1))
        for bit in bits:
            place = bit.bit_length() - 1
            low = 1
            for p in left:
                low *= 2 if p < place else 1
            left.remove(place)
            blocks = blocks.reshape(-1, 2, low, rows, blocks.shape[-1])
            mine = (copy >> place) & 1
            keep = lax.dynamic_index_in_dim(blocks, mine, 1, keepdims=False)
            give = lax.dynamic_index_in_dim(blocks, 1 - mine, 1, keepdims=False)
            come = flip(give, "dp", bit)
            blocks = (keep.astype(jnp.float32) + come.astype(jnp.float32)).astype(jnp.bfloat16)
            blocks = blocks.reshape(-1, rows, blocks.shape[-1])
        return blocks[0]

    def scatter_copies(whole):
        return lax.psum_scatter(whole, "dp", scatter_dimension=0, tiled=True)

    def reduce_ranks(blocks):
        return sum(g.astype(jnp.float32) for g in exchange(blocks))

    context_grad, outer_whole, inner_whole, output_whole = lax.optimization_barrier(
        (context_grad, outer_whole, inner_whole, output_whole)
    )
    outer_rows = scatter_copies(outer_whole)
    outer_weight_grad = reduce_ranks(jnp.split(outer_rows, ranks, axis=1))
    both_rows = reduce_copies(jnp.concatenate([inner_whole, output_whole], axis=1))
    inner_rows = jnp.split(both_rows[:, : ranks * units], ranks, axis=1)
    output_rows = jnp.split(both_rows[:, ranks * units :], ranks, axis=1)
    both_sum = reduce_ranks(
        [jnp.concatenate([i, o], axis=1) for i, o in zip(inner_rows, output_rows)]
    )
    inner_weight_grad, output_weight_grad = both_sum[:, :units], both_sum[:, units:]

    input_rows = first_grad
    qkv_sums, query_sums = [], []
    for pair in range(pairs):
        qkv_low = attend_backward(lengths, extended[pair], qkv, contexts[pair], context_grad, pair)
        columns = slice(3 * PAIR * pair, 3 * PAIR * (pair + 1))
        for block, weight in zip(exchange(spread(qkv_low)), qkv_weights):
            input_rows = input_rows + times_rows(block, weight[:, columns])
        whole = over_rows(hidden_in, qkv_low).astype(jnp.bfloat16)
        qkv_sums.append(scatter_copies(whole) if pair == 0 else reduce_copies(whole))
        query_sums.append(jnp.sum(qkv_low[:, :PAIR].astype(jnp.float32), axis=0))
    qkv_sums = [jnp.split(w.astype(jnp.float32), 3, axis=1) for w in qkv_sums]
    query_weight_grad, key_weight_grad, value_weight_grad = [
        jnp.concatenate([w[i] for w in qkv_sums], axis=1) for i in range(3)
    ]

    def column_sums(array_in):
        return jnp.sum(array_in.astype(jnp.float32), axis=0)

    vectors = [
        ordered(column_sums(inner_low_all)),
        column_sums(attention_low),
        column_sums(normed_grad * normal_one),
        column_sums(normed_grad),
        column_sums(branch_low),
        column_sums(final_grad * normal_two),
        column_sums(final_grad),
        ordered(column_sums(grad_all)),
        jnp.full((model_width,), loss_part),
    ]
    vectors = jnp.concatenate(vectors).reshape(-1, model_width)
    vectors = jnp.sum(lax.all_gather(vectors, ("dp", "tensor")), axis=0)
    wide = ranks * units // model_width
    inner_bias_grad = vectors[:wide].reshape(-1)
    (
        output_bias_grad,
        first_gain_grad,
        first_shift_grad,
        outer_bias_grad,
        second_gain_grad,
        second_shift_grad,
        value_bias_grad,
    ) = [vectors[wide + i] for i in range(7)]
    query_bias_grad = lax.dynamic_update_slice_in_dim(
        jnp.zeros((model_width,), jnp.float32), jnp.concatenate(query_sums), rank * heads_width, 0
    )
    query_bias_grad = total(query_bias_grad, ("dp", "tensor"))
    return (
        final.astype(jnp.bfloat16),
        vectors[wide + 7, 0] / token_total,
        input_rows,
        query_weight_grad,
        query_bias_grad,
        key_weight_grad,
        value_weight_grad,
        value_bias_grad,
        output_weight_grad,
        output_bias_grad,
        first_gain_grad,
        first_shift_grad,
        inner_weight_grad,
        inner_bias_grad,
        outer_weight_grad,
        outer_bias_grad,
        second_gain_grad,
        second_shift_grad,
    )


def solution(mesh):
    rows, columns, split = P("dp", None), P(None, "tensor"), P("dp", "tensor")
    part, whole, own = P("tensor"), P(), P(("dp", "tensor"), None)
    in_specs = (
        rows,
        P("dp"),
        columns,
        part,
        columns,
        columns,
        part,
        columns,
        whole,
        whole,
        whole,
        columns,
        part,
        columns,
        whole,
        whole,
        whole,
        rows,
        rows,
    )
    out_specs = (
        own,
        whole,
        own,
        split,
        whole,
        split,
        split,
        whole,
        split,
        whole,
        whole,
        whole,
        split,
        whole,
        split,
        whole,
        whole,
        whole,
    )
    return jax.shard_map(shards, mesh=mesh, in_specs=in_specs, out_specs=out_specs, check_vma=False)
```

time: 833 us -> 584 us (0.70)
  matrix products: 268 us -> 96.6 us
  waiting for transfers between devices: 318 us -> 190 us
  Pallas kernels: 0 us -> 90.4 us
  other arithmetic: 92.9 us -> 37.3 us
  local copies, waits for them, and re-layouts: 52.1 us -> 67.5 us
    reduce_scatter x4 -> x1, waiting for transfers between devices: 236 us -> 0.02 us  [scatter_copies(): return lax.psum_scatter(whole, 'dp', scatter_dimension=0, tiled=True)]
    dot_general x28 -> x0, matrix products: 172 us -> none  [the longest x4 43.8 us: one_block(): jnp.einsum('qhd,khd->hqk', grad_block, values_split, preferred_element_ty...]
    ppermute x40 -> x47, waiting for transfers between devices: 82.2 us -> 190 us  [flip(): lax.ppermute(array_in, axis_name, [(i, i ^ bits) for i in range(size)])]
    pallas_call x0 -> x4, Pallas kernels: none -> 90.4 us  [the longest x2 57.9 us: attend_backward(): pl.pallas_call(backward_kernel, grid_spec=pltpu.PrefetchScalarGridSpec(nu...]
    convert_element_type x7 -> x6, other arithmetic: 42.8 us -> 11.4 us  [the longest x4 11.4 us: reduce_copies(): (keep.astype(jnp.float32) + come.astype(jnp.float32)).astype(jnp.bfloat16)]
    squeeze x0 -> x6, local copies, waits for them, and re-layouts: none -> 14 us  [the longest x2 8.22 us: gather(): return [weight] + [others[s] for s in range(ranks - 1)]]
    dot_general x15 -> x10, matrix products: 36.7 us -> 24.9 us  [matmul(): return jnp.dot(former, latter, preferred_element_type=jnp.float32)]
    reduce_sum x4 -> x3, other arithmetic: 15 us -> 3.33 us  [the longest x1 1.72 us: shards(): vectors = jnp.sum(lax.all_gather(vectors, ('dp', 'tensor')), axis=0)]
  transfers between devices with their start and end apart: 48 -> 53, of which waited for: 25 -> 18; matrix products, arithmetic and copies ran while one was open for 19% -> 32% of each run, Pallas kernels for 0% -> 16%
where the time goes in v2:
time: 584 us; the launch traced here: 573 us
  waiting for transfers between devices  190 us (33%)
  matrix products  96.6 us (17%)
  Pallas kernels  90.4 us (15%)
  starting transfers between devices  71.3 us (12%)
  local copies, waits for them, and re-layouts  67.5 us (12%)
  other arithmetic  37.3 us (6%)
  between operations  20.3 us (3%)
    ppermute x47, waiting for transfers between devices, flip(): lax.ppermute(array_in, axis_name, [(i, i ^ bits) for i in range(size)])  190 us
    ppermute x47, starting transfers between devices, flip(): lax.ppermute(array_in, axis_name, [(i, i ^ bits) for i in range(size)])  70.6 us
    pallas_call x2, Pallas kernels, attend_backward(): pl.pallas_call(backward_kernel, grid_spec=pltpu.PrefetchScalarGridSpec(nu...  57.9 us
    dot_general x17, matrix products, times_rows(): lax.dot_general(former, latter, (((1,), (1,)), ((), ())), preferred_eleme...  43.1 us
    pallas_call x2, Pallas kernels, attend_forward(): pl.pallas_call(forward_kernel, grid_spec=pltpu.PrefetchScalarGridSpec(num...  32.5 us
    unnamed x192, local copies, waits for them, and re-layouts  28.8 us
    dot_general x5, matrix products, over_rows(): lax.dot_general(former, latter, (((0,), (0,)), ((), ())), preferred_eleme...  28.6 us
    dot_general x10, matrix products, matmul(): return jnp.dot(former, latter, preferred_element_type=jnp.float32)  24.9 us
  transfers between devices with their start and end apart: 53, of which 18 were waited for; matrix products, arithmetic and copies ran while one was open for 32% of the time, Pallas kernels for 16%

profile of v2, /device:TPU:0, one launch (start us, length us, event | category | flops | bytes accessed | tf_op | source)
XLA Modules:
  0.0 573.0 jit_solution(388707801383034160)
XLA Ops:
  14.1 11.4 %collective-permute-done.6 = bf16[128,1280]{1,0:T(8,128)(2,1)S(1)} collective-permute-done((bf16[128,1280]{1,0:T(8,128)(2,1)S(1)}, bf16[128,1280]{1,0:T(8,128)(2,1)S(1)}, u32[]{:S(2)}, u32[]{:S(2)}) %collective-permute-start.6) | collective-permute-done | bytes 327712 | tf_op jit(solution)/shard_map/ppermute | solution.py:238
  25.5 11.5 %collective-permute-done.7 = bf16[128,1280]{1,0:T(8,128)(2,1)S(1)} collective-permute-done((bf16[128,1280]{1,0:T(8,128)(2,1)S(1)}, bf16[128,1280]{1,0:T(8,128)(2,1)S(1)}, u32[]{:S(2)}, u32[]{:S(2)}) %collective-permute-start.7) | collective-permute-done | bytes 327712 | tf_op jit(solution)/shard_map/ppermute | solution.py:238
  38.2 6.3 %collective-permute-start.10 = (bf16[128,1024]{1,0:T(8,128)(2,1)S(1)}, bf16[128,1024]{1,0:T(8,128)(2,1)S(1)}, u32[]{:S(2)}, u32[]{:S(2)}) collective-permute-start(bf16[128,1024]{1,0:T(8,128)(2,1)S(1)} %constant_dynamic-slice_fusion.21), channel_id=1, source_target_pairs={{0,1},{1,0},{2,3},{3,2},{4,5},{5,4},{6,7},{7,6},{8,9},{9,8},{10,11... | collective-permute-start | bytes 786440 | tf_op jit(solution)/shard_map/ppermute | solution.py:238
  47.0 7.0 %collective-permute-done.10 = bf16[128,1024]{1,0:T(8,128)(2,1)S(1)} collective-permute-done((bf16[128,1024]{1,0:T(8,128)(2,1)S(1)}, bf16[128,1024]{1,0:T(8,128)(2,1)S(1)}, u32[]{:S(2)}, u32[]{:S(2)}) %collective-permute-start.10) | collective-permute-done | bytes 262176 | tf_op jit(solution)/shard_map/ppermute | solution.py:238
  54.0 11.9 %collective-permute-done.11 = bf16[128,1024]{1,0:T(8,128)(2,1)S(1)} collective-permute-done((bf16[128,1024]{1,0:T(8,128)(2,1)S(1)}, bf16[128,1024]{1,0:T(8,128)(2,1)S(1)}, u32[]{:S(2)}, u32[]{:S(2)}) %collective-permute-start.11) | collective-permute-done | bytes 262176 | tf_op jit(solution)/shard_map/ppermute | solution.py:238
  77.2 4.7 fusion.9.q_ref.k_ref.v_ref
  82.0 16.2 %attend_forward.2 = (bf16[2048,128]{1,0:T(8,128)(2,1)}, bf16[2,2048,128]{2,1,0:T(8,128)(2,1)}) custom-call(s32[1]{0:T(128)} %copy.109.length_ref, bf16[2048,768]{1,0:T(8,128)(2,1)} %fusion.9.q_ref.k_ref.v_ref, bf16[2048,768]{1,0:T(8,128)(2,1)} %fusion.9.q_ref.k_ref.v_ref, bf16[2048,768]{1,0:T(8,128)(2,1)} %fusion.9.q_ref.k_ref.v_ref), custom_call_target="tpu_custom_call" | custom-call | flops 8589934592 | bytes 3145728 | tf_op jit(solution)/shard_map/attend_forward/pallas_call | solution.py:114
  102.1 16.3 %attend_forward.3 = (bf16[2048,128]{1,0:T(8,128)(2,1)}, bf16[2,2048,128]{2,1,0:T(8,128)(2,1)}) custom-call(s32[1]{0:T(128)} %copy.109.length_ref, bf16[2048,768]{1,0:T(8,128)(2,1)} %fusion.9.q_ref.k_ref.v_ref, bf16[2048,768]{1,0:T(8,128)(2,1)} %fusion.9.q_ref.k_ref.v_ref, bf16[2048,768]{1,0:T(8,128)(2,1)} %fusion.9.q_ref.k_ref.v_ref), custom_call_target="tpu_custom_call" | custom-call | flops 8589934592 | bytes 3145728 | tf_op jit(solution)/shard_map/attend_forward/pallas_call | solution.py:114
  140.0 21.1 %collective-permute-done.2 = bf16[512,128]{1,0:T(8,128)(2,1)S(1)} collective-permute-done((bf16[512,128]{1,0:T(8,128)(2,1)S(1)}, bf16[512,128]{1,0:T(8,128)(2,1)S(1)}, u32[]{:S(2)}, u32[]{:S(2)}) %collective-permute-start.2) | collective-permute-done | bytes 131104 | tf_op jit(solution)/shard_map/ppermute | solution.py:238
  210.1 4.7 multiply_reduce_fusion
  248.3 7.4 %convolution_convert_fusion = bf16[1024,4096]{1,0:T(8,128)(2,1)} fusion(bf16[512,1024]{1,0:T(8,128)(2,1)S(1)} %copy-done.32, bf16[512,1024]{1,0:T(8,128)(2,1)S(1)} %copy-done.39, bf16[512,1024]{1,0:T(8,128)(2,1)S(1)} %copy-done.37, bf16[512,1024]{1,0:T(8,128)(2,1)S(1)} %multiply_convert_fusion.2, bf16[512,1024]{1,0:T(8,128)(2,1)S(1)} %copy-done.41), kind=kOutput, calls=%fused_computation.4 | convolution fusion | flops 4315938816 | bytes 13631488 | tf_op jit(solution)/shard_map/dot_general | solution.py:27
  255.7 7.4 %convolution_convert_fusion.1 = bf16[1024,4096]{1,0:T(8,128)(2,1)} fusion(bf16[512,1024]{1,0:T(8,128)(2,1)S(1)} %copy-done.30, bf16[512,1024]{1,0:T(8,128)(2,1)S(1)} %copy-done.68, bf16[512,1024]{1,0:T(8,128)(2,1)S(1)} %copy-done.77, bf16[512,1024]{1,0:T(8,128)(2,1)S(1)} %copy-done.75, bf16[512,1024]{1,0:T(8,128)(2,1)S(1)} %copy-done.71), kind=kOutput, calls=%fused_computation.5 | convolution fusion | flops 4315938816 | bytes 13631488 | tf_op jit(solution)/shard_map/dot_general | solution.py:27
  267.1 29.0 %attend_backward.2 = bf16[2048,384]{1,0:T(8,128)(2,1)} custom-call(s32[1]{0:T(128)} %copy.109.length_ref, bf16[2,2048,128]{2,1,0:T(8,128)(2,1)} %get-tuple-element.28.extended_ref, bf16[2048,768]{1,0:T(8,128)(2,1)} %fusion.9.q_ref.k_ref.v_ref, bf16[2048,768]{1,0:T(8,128)(2,1)} %fusion.9.q_ref.k_ref.v_ref, bf16[2048,128]{1,0:T(8,128)(2,1)} %get-tuple-element.26.context_ref, ...), custom_call_target="tpu_custom_call" | custom-call | flops 21474836480 | bytes 5242880 | tf_op jit(solution)/shard_map/attend_backward/pallas_call | solution.py:207
  303.3 5.6 pad_maximum_fusion
  319.2 28.9 %attend_backward.3 = bf16[2048,384]{1,0:T(8,128)(2,1)} custom-call(s32[1]{0:T(128)} %copy.109.length_ref, bf16[2,2048,128]{2,1,0:T(8,128)(2,1)} %get-tuple-element.30.extended_ref, bf16[2048,768]{1,0:T(8,128)(2,1)} %fusion.9.q_ref.k_ref.v_ref, bf16[2048,768]{1,0:T(8,128)(2,1)} %fusion.9.q_ref.k_ref.v_ref, bf16[2048,128]{1,0:T(8,128)(2,1)} %get-tuple-element.27.context_ref, ...), custom_call_target="tpu_custom_call" | custom-call | flops 21474836480 | bytes 5242880 | tf_op jit(solution)/shard_map/attend_backward/pallas_call | solution.py:207
  350.3 5.4 fusion.52
  366.0 6.1 %fusion = bf16[4,1,128,5120]{3,2,0,1:T(8,128)(2,1)S(1)} fusion(bf16[4,1,128,5120]{3,2,0,1:T(8,128)(2,1)} %collective-permute-done.38, bf16[4,2,1,128,5120]{4,3,1,0,2:T(8,128)(2,1)} %bitcast.141, s32[]{:T(128)S(6)} %select_n.106), kind=kLoop, calls=%fused_computation.2 | loop fusion | flops 10485760 | bytes 15728644 | tf_op jit(solution)/shard_map/convert_element_type | solution.py:396
  384.1 11.9 %collective-permute-done.36 = f32[1024]{0:T(1024)S(1)} collective-permute-done((f32[1024]{0:T(1024)S(1)}, f32[1024]{0:T(1024)S(1)}, u32[]{:S(2)}, u32[]{:S(2)}) %collective-permute-start.36) | collective-permute-done | bytes 4128 | tf_op jit(solution)/shard_map/ppermute | solution.py:238
  415.3 31.8 %collective-permute-done.25 = bf16[512,384]{1,0:T(8,128)(2,1)} collective-permute-done((bf16[512,384]{1,0:T(8,128)(2,1)}, bf16[512,384]{1,0:T(8,128)(2,1)}, u32[]{:S(2)}, u32[]{:S(2)}) %collective-permute-start.25) | collective-permute-done | bytes 393248 | tf_op jit(solution)/shard_map/ppermute | solution.py:238
  452.8 11.2 %collective-permute-done.28 = bf16[512,384]{1,0:T(8,128)(2,1)} collective-permute-done((bf16[512,384]{1,0:T(8,128)(2,1)S(1)}, bf16[512,384]{1,0:T(8,128)(2,1)}, u32[]{:S(2)}, u32[]{:S(2)}) %collective-permute-start.28) | collective-permute-done | bytes 393248 | tf_op jit(solution)/shard_map/ppermute | solution.py:238
  485.2 25.9 %collective-permute-done.40 = bf16[1,1,128,5120]{3,2,1,0:T(8,128)(2,1)S(1)} collective-permute-done((bf16[1,1,128,5120]{3,2,1,0:T(8,128)(2,1)}, bf16[1,1,128,5120]{3,2,1,0:T(8,128)(2,1)S(1)}, u32[]{:S(2)}, u32[]{:S(2)}) %collective-permute-start.40) | collective-permute-done | bytes 1310752 | tf_op jit(solution)/shard_map/ppermute | solution.py:238
  523.4 7.2 %collective-permute-done.41 = bf16[128,1280]{1,0:T(8,128)(2,1)S(1)} collective-permute-done((bf16[128,1280]{1,0:T(8,128)(2,1)S(1)}, bf16[128,1280]{1,0:T(8,128)(2,1)S(1)}, u32[]{:S(2)}, u32[]{:S(2)}) %collective-permute-start.41) | collective-permute-done | bytes 327712 | tf_op jit(solution)/shard_map/ppermute | solution.py:238
  532.3 6.8 %collective-permute-done.42 = bf16[128,1280]{1,0:T(8,128)(2,1)S(1)} collective-permute-done((bf16[128,1280]{1,0:T(8,128)(2,1)S(1)}, bf16[128,1280]{1,0:T(8,128)(2,1)S(1)}, u32[]{:S(2)}, u32[]{:S(2)}) %collective-permute-start.42) | collective-permute-done | bytes 327712 | tf_op jit(solution)/shard_map/ppermute | solution.py:238
  541.4 21.6 %collective-permute-done.45 = bf16[128,1024]{1,0:T(8,128)(2,1)S(1)} collective-permute-done((bf16[128,1024]{1,0:T(8,128)(2,1)S(1)}, bf16[128,1024]{1,0:T(8,128)(2,1)S(1)}, u32[]{:S(2)}, u32[]{:S(2)}) %collective-permute-start.45) | collective-permute-done | bytes 262176 | tf_op jit(solution)/shard_map/ppermute | solution.py:238
  (420 shorter events, 235.6 us)
Async XLA Ops:
  7.2 169.8 %all-gather.5.cloned.1.call-start = ((), (), s32[]{:S(2)}) async-start(), calls=%async_computation.2 | async-start | bytes 8847360 | tf_op jit(solution)/shard_map/all_gather | solution.py:297
  38.1 163.0 %all-gather.7.cloned.1.call-start = ((), (), s32[]{:S(2)}) async-start(), calls=%async_computation.3 | async-start | bytes 7077888 | tf_op jit(solution)/shard_map/all_gather | solution.py:297
  66.8 247.7 %all-gather.11.cloned.1.call-start = ((), (), s32[]{:S(2)}) async-start(), calls=%async_computation.5 | async-start | bytes 5308416 | tf_op jit(solution)/shard_map/all_gather | solution.py:297
  66.9 64.3 %collective-permute-start.9 = (bf16[1024]{0:T(1024)(128)(2,1)S(1)}, bf16[1024]{0:T(1024)(128)(2,1)S(1)}, u32[]{:S(2)}, u32[]{:S(2)}) collective-permute-start(bf16[1024]{0:T(1024)(128)(2,1)S(1)} %copy-done.61), channel_id=1, source_target_pairs={{0,1},{1,0},{2,3},{3,2},{4,5},{5,4},{6,7},{7,6},{8,9},{9,8},{10,11... | collective-permute-start | bytes 6152 | tf_op jit(solution)/shard_map/ppermute | solution.py:238
  70.7 61.6 %collective-permute-start.13 = (bf16[1024]{0:T(1024)(128)(2,1)S(1)}, bf16[1024]{0:T(1024)(128)(2,1)S(1)}, u32[]{:S(2)}, u32[]{:S(2)}) collective-permute-start(bf16[1024]{0:T(1024)(128)(2,1)S(1)} %copy-done.61), channel_id=1, source_target_pairs={{0,2},{1,3},{2,0},{3,1},{4,6},{5,7},{6,4},{7,5},{8,10},{9,11},{10,... | collective-permute-start | bytes 6152 | tf_op jit(solution)/shard_map/ppermute | solution.py:238
  71.7 48.5 %collective-permute-start.15 = (s32[1]{0:T(128)}, s32[1]{0:T(128)}, u32[]{:S(2)}, u32[]{:S(2)}) collective-permute-start(s32[1]{0:T(128)} %param.20), channel_id=1, source_target_pairs={{0,4},{4,0},{8,12},{12,8},{16,20},{20,16},{24,28},{28,24},{1,5},{5... | collective-permute-start | bytes 20 | tf_op jit(solution)/shard_map/ppermute | solution.py:238
  100.0 35.7 %collective-permute-start = (bf16[512,128]{1,0:T(8,128)(2,1)S(1)}, bf16[512,128]{1,0:T(8,128)(2,1)S(1)}, u32[]{:S(2)}, u32[]{:S(2)}) collective-permute-start(bf16[512,128]{1,0:T(8,128)(2,1)S(1)} %get-tuple-element.165), channel_id=1, source_target_pairs={{0,1},{1,0},{2,3},{3,2},{4,5},{5,4},{6,7},{7,6},{8,9},{9,8},{10,11... | collective-permute-start | bytes 393224 | tf_op jit(solution)/shard_map/ppermute | solution.py:238
  131.1 44.4 %collective-permute-start.22 = (bf16[128,768]{1,0:T(8,128)(2,1)S(1)}, bf16[128,768]{1,0:T(8,128)(2,1)S(1)}, u32[]{:S(2)}, u32[]{:S(2)}) collective-permute-start(bf16[128,768]{1,0:T(8,128)(2,1)S(1)} %constant_dynamic-slice_fusion.11), channel_id=1, source_target_pairs={{0,1},{1,0},{2,3},{3,2},{4,5},{5,4},{6,7},{7,6},{8,9},{9,8},{10,11... | collective-permute-start | bytes 589832 | tf_op jit(solution)/shard_map/ppermute | solution.py:238
  132.3 43.3 %collective-permute-start.23 = (bf16[128,768]{1,0:T(8,128)(2,1)S(1)}, bf16[128,768]{1,0:T(8,128)(2,1)S(1)}, u32[]{:S(2)}, u32[]{:S(2)}) collective-permute-start(bf16[128,768]{1,0:T(8,128)(2,1)S(1)} %constant_dynamic-slice_fusion.11), channel_id=1, source_target_pairs={{0,2},{1,3},{2,0},{3,1},{4,6},{5,7},{6,4},{7,5},{8,10},{9,11},{10,... | collective-permute-start | bytes 589832 | tf_op jit(solution)/shard_map/ppermute | solution.py:238
  134.4 41.1 %collective-permute-start.24 = (bf16[128,768]{1,0:T(8,128)(2,1)S(1)}, bf16[128,768]{1,0:T(8,128)(2,1)S(1)}, u32[]{:S(2)}, u32[]{:S(2)}) collective-permute-start(bf16[128,768]{1,0:T(8,128)(2,1)S(1)} %constant_dynamic-slice_fusion.11), channel_id=1, source_target_pairs={{0,3},{1,2},{2,1},{3,0},{4,7},{5,6},{6,5},{7,4},{8,11},{9,10},{10,... | collective-permute-start | bytes 589832 | tf_op jit(solution)/shard_map/ppermute | solution.py:238
  176.5 303.1 %reduce-scatter.7.cloned.1.call-start = ((), (), s32[]{:S(2)}) async-start(), calls=%async_computation.7 | async-start | bytes 884736
  301.7 181.1 %all-gather.9.cloned.1.call-start = ((), (), s32[]{:S(2)}) async-start(), calls=%async_computation.4 | async-start | bytes 2162688 | tf_op jit(solution)/shard_map/all_gather | solution.py:449
  303.2 216.1 %reduce-scatter.5.cloned.1.call-start = ((), (), s32[]{:S(2)}) async-start(), calls=%async_computation.6 | async-start | bytes 9437184 | tf_op jit(solution)/shard_map/reduce_scatter | solution.py:401
  314.5 51.5 %collective-permute-start.38 = (bf16[4,1,128,5120]{3,2,0,1:T(8,128)(2,1)}, bf16[4,1,128,5120]{3,2,0,1:T(8,128)(2,1)}, u32[]{:S(2)}, u32[]{:S(2)}) collective-permute-start(bf16[4,1,128,5120]{3,2,0,1:T(8,128)(2,1)} %dynamic-slice_bitcast_fusion), channel_id=1, source_target_pairs={{0,4},{4,0},{8,12},{12,8},{16,20},{20,16},{24,28},{28,24},{1,5},{5... | collective-permute-start | bytes 15728648 | tf_op jit(solution)/shard_map/ppermute | solution.py:238
  359.7 43.6 %collective-permute-start.21 = (bf16[512,384]{1,0:T(8,128)(2,1)}, bf16[512,384]{1,0:T(8,128)(2,1)}, u32[]{:S(2)}, u32[]{:S(2)}) collective-permute-start(bf16[512,384]{1,0:T(8,128)(2,1)} %get-tuple-element.130), channel_id=1, source_target_pairs={{0,1},{1,0},{2,3},{3,2},{4,5},{5,4},{6,7},{7,6},{8,9},{9,8},{10,11... | collective-permute-start | bytes 1179656 | tf_op jit(solution)/shard_map/ppermute | solution.py:238
  375.2 92.8 %collective-permute-start.39 = (bf16[1,2,128,5120]{3,2,1,0:T(8,128)(2,1)}, bf16[1,2,128,5120]{3,2,1,0:T(8,128)(2,1)}, u32[]{:S(2)}, u32[]{:S(2)}) collective-permute-start(bf16[1,2,128,5120]{3,2,1,0:T(8,128)(2,1)} %dynamic-slice_bitcast_fusion.1), channel_id=1, source_target_pairs={{0,16},{4,20},{8,24},{12,28},{16,0},{20,4},{24,8},{28,12},{1,17},{... | collective-permute-start | bytes 7864328 | tf_op jit(solution)/shard_map/ppermute | solution.py:238
  378.5 34.6 %collective-permute-start.30 = (bf16[4,1,128,384]{3,2,0,1:T(8,128)(2,1)}, bf16[4,1,128,384]{3,2,0,1:T(8,128)(2,1)}, u32[]{:S(2)}, u32[]{:S(2)}) collective-permute-start(bf16[4,1,128,384]{3,2,0,1:T(8,128)(2,1)} %bitcast.145), channel_id=1, source_target_pairs={{0,4},{4,0},{8,12},{12,8},{16,20},{20,16},{24,28},{28,24},{1,5},{5... | collective-permute-start | bytes 1179656 | tf_op jit(solution)/shard_map/ppermute | solution.py:238
  401.0 46.2 %collective-permute-start.25 = (bf16[512,384]{1,0:T(8,128)(2,1)}, bf16[512,384]{1,0:T(8,128)(2,1)}, u32[]{:S(2)}, u32[]{:S(2)}) collective-permute-start(bf16[512,384]{1,0:T(8,128)(2,1)} %get-tuple-element.132), channel_id=1, source_target_pairs={{0,2},{1,3},{2,0},{3,1},{4,6},{5,7},{6,4},{7,5},{8,10},{9,11},{10,... | collective-permute-start | bytes 1179656 | tf_op jit(solution)/shard_map/ppermute | solution.py:238
  403.3 62.7 %collective-permute-start.26 = (bf16[512,384]{1,0:T(8,128)(2,1)}, bf16[512,384]{1,0:T(8,128)(2,1)}, u32[]{:S(2)}, u32[]{:S(2)}) collective-permute-start(bf16[512,384]{1,0:T(8,128)(2,1)} %get-tuple-element.131), channel_id=1, source_target_pairs={{0,3},{1,2},{2,1},{3,0},{4,7},{5,6},{6,5},{7,4},{8,11},{9,10},{10,... | collective-permute-start | bytes 1179656 | tf_op jit(solution)/shard_map/ppermute | solution.py:238
  408.8 55.2 %collective-permute-start.28 = (bf16[512,384]{1,0:T(8,128)(2,1)S(1)}, bf16[512,384]{1,0:T(8,128)(2,1)}, u32[]{:S(2)}, u32[]{:S(2)}) collective-permute-start(bf16[512,384]{1,0:T(8,128)(2,1)S(1)} %copy-done.53), channel_id=1, source_target_pairs={{0,2},{1,3},{2,0},{3,1},{4,6},{5,7},{6,4},{7,5},{8,10},{9,11},{10,... | collective-permute-start | bytes 1179656 | tf_op jit(solution)/shard_map/ppermute | solution.py:238
  413.1 62.1 %collective-permute-start.29 = (bf16[512,384]{1,0:T(8,128)(2,1)}, bf16[512,384]{1,0:T(8,128)(2,1)}, u32[]{:S(2)}, u32[]{:S(2)}) collective-permute-start(bf16[512,384]{1,0:T(8,128)(2,1)} %get-tuple-element.127), channel_id=1, source_target_pairs={{0,3},{1,2},{2,1},{3,0},{4,7},{5,6},{6,5},{7,4},{8,11},{9,10},{10,... | collective-permute-start | bytes 1179656 | tf_op jit(solution)/shard_map/ppermute | solution.py:238
  473.4 37.7 %collective-permute-start.40 = (bf16[1,1,128,5120]{3,2,1,0:T(8,128)(2,1)}, bf16[1,1,128,5120]{3,2,1,0:T(8,128)(2,1)S(1)}, u32[]{:S(2)}, u32[]{:S(2)}) collective-permute-start(bf16[1,1,128,5120]{3,2,1,0:T(8,128)(2,1)} %constant_dynamic-slice_fusion), channel_id=1, source_target_pairs={{0,8},{4,12},{8,0},{12,4},{16,24},{20,28},{24,16},{28,20},{1,9},{5... | collective-permute-start | bytes 3932168 | tf_op jit(solution)/shard_map/ppermute | solution.py:238
  520.6 42.3 %collective-permute-start.45 = (bf16[128,1024]{1,0:T(8,128)(2,1)S(1)}, bf16[128,1024]{1,0:T(8,128)(2,1)S(1)}, u32[]{:S(2)}, u32[]{:S(2)}) collective-permute-start(bf16[128,1024]{1,0:T(8,128)(2,1)S(1)} %get-tuple-element.143), channel_id=1, source_target_pairs={{0,2},{1,3},{2,0},{3,1},{4,6},{5,7},{6,4},{7,5},{8,10},{9,11},{10,... | collective-permute-start | bytes 786440 | tf_op jit(solution)/shard_map/ppermute | solution.py:238
  530.6 32.4 %collective-permute-start.46 = (bf16[128,1024]{1,0:T(8,128)(2,1)S(1)}, bf16[128,1024]{1,0:T(8,128)(2,1)S(1)}, u32[]{:S(2)}, u32[]{:S(2)}) collective-permute-start(bf16[128,1024]{1,0:T(8,128)(2,1)S(1)} %get-tuple-element.142), channel_id=1, source_target_pairs={{0,3},{1,2},{2,1},{3,0},{4,7},{5,6},{6,5},{7,4},{8,11},{9,10},{10,... | collective-permute-start | bytes 786440 | tf_op jit(solution)/shard_map/ppermute | solution.py:238
  (107 other events, 1306.9 us)
Sparse Core Ops, SparseCore 0:
  38.2 56.9 all-gather.4
  97.1 45.4 all-gather.6
  176.6 38.4 all-gather.10
  301.9 34.5 reduce-scatter.6
  339.8 59.3 all-gather.8
  402.6 90.0 reduce-scatter.4

commit v3 on v2

--- a/solution.py
+++ b/solution.py
@@ -233,6 +233,10 @@
     )(length, extended, qkv, qkv, context, context_grad)
 
 
+def tie(*values):
+    return lax.optimization_barrier(values)
+
+
 def flip(array_in, axis_name, bits):
     size = lax.axis_size(axis_name)
     return lax.ppermute(array_in, axis_name, [(i, i ^ bits) for i in range(size)])
@@ -287,15 +291,15 @@
             [a[..., p * PAIR : (p + 1) * PAIR] for p in range(pairs) for a in arrays], axis=-1
         )
 
-    qkv_weight = by_pairs(query_weight, key_weight, value_weight)
-    qkv_bias = by_pairs(query_bias, jnp.zeros_like(query_bias), value_bias)
-
-    def gather(weight):
+    def own_part(weight):
         rows = weight.shape[0] // copies
-        part = lax.dynamic_slice_in_dim(weight, copy * rows, rows, 0)
-        others = jnp.stack([flip(part, "tensor", s) for s in range(1, ranks)])
-        others = lax.all_gather(others, "dp", axis=1, tiled=True)
-        return [weight] + [others[s] for s in range(ranks - 1)]
+        return lax.dynamic_slice_in_dim(weight, copy * rows, rows, 0)
+
+    def others(part):
+        return jnp.stack([flip(part, "tensor", s) for s in range(1, ranks)])
+
+    def gathered(parts):
+        return lax.all_gather(parts, "dp", axis=1, tiled=True)
 
     def spread(array_in):
         own = []
@@ -307,29 +311,89 @@
     def exchange(blocks):
         return [blocks[0]] + [flip(blocks[s], "tensor", s) for s in range(1, ranks)]
 
+    def reduce_ranks(blocks):
+        return sum(g.astype(jnp.float32) for g in exchange(blocks))
+
     def ordered(vector_in):
         table = vector_in.reshape(ranks, -1)
         return jnp.concatenate(
             [lax.dynamic_index_in_dim(table, rank ^ s, 0, keepdims=False) for s in range(ranks)]
         )
 
-    early = gather(jnp.concatenate([inner_weight, output_weight], axis=1))
-    inner_weights = [w[:, :units] for w in early]
-    output_weight_all = jnp.concatenate([w[:, units:] for w in early], axis=1)
-    outer_weights = gather(outer_weight)
-    qkv_weights = gather(qkv_weight)
-    inner_biases = [inner_bias] + [flip(inner_bias, "tensor", s) for s in range(1, ranks)]
+    def half_columns(array_in, other):
+        blocks = array_in.reshape(array_in.shape[0], copies // 2, 2, -1)
+        mine = lax.dynamic_index_in_dim(blocks, (copy & 1) ^ other, 2, keepdims=False)
+        return mine.reshape(array_in.shape[0], -1)
+
+    def first_give(former, latter):
+        return over_rows(half_columns(former, 1), latter).astype(jnp.bfloat16)
+
+    def first_keep(former, latter, come):
+        kept = over_rows(half_columns(former, 0), latter) + come.astype(jnp.float32)
+        return kept.astype(jnp.bfloat16)
+
+    def high_steps(kept):
+        rows = model_width // copies
+        places = list(range(1, copies.bit_length() - 1))
+        half = kept.shape[1] // 2
+        halves = []
+        for part, order in ((kept[:, :half], places[::-1]), (kept[:, half:], places)):
+            blocks = part.reshape(-1, rows, half)
+            left = list(places)
+            for place in order:
+                low = 2 ** sum(p < place for p in left)
+                left.remove(place)
+                blocks = blocks.reshape(-1, 2, low, rows, half)
+                mine = (copy >> place) & 1
+                keep = lax.dynamic_index_in_dim(blocks, mine, 1, keepdims=False)
+                give = lax.dynamic_index_in_dim(blocks, 1 - mine, 1, keepdims=False)
+                come = flip(give, "dp", 1 << place)
+                blocks = keep.astype(jnp.float32) + come.astype(jnp.float32)
+                blocks = blocks.astype(jnp.bfloat16).reshape(-1, rows, half)
+            halves.append(blocks[0])
+        return jnp.concatenate(halves, axis=1)
+
+    def scatter_copies(whole):
+        return lax.psum_scatter(whole, "dp", scatter_dimension=0, tiled=True)
+
+    def column_sums(array_in):
+        return jnp.sum(array_in.astype(jnp.float32), axis=0)
+
+    qkv_weight = by_pairs(query_weight, key_weight, value_weight)
+    qkv_bias = by_pairs(query_bias, jnp.zeros_like(query_bias), value_bias)
     token_total = total(lengths, ("dp",))[0].astype(jnp.float32)
     grad_scale = seq_len * copies / (2.0 * token_total)
-
+    first_part = own_part(jnp.concatenate([inner_weight, output_weight], axis=1))
+    later_part = own_part(jnp.concatenate([outer_weight, qkv_weight], axis=1))
+    first_parts = others(first_part)
     qkv = (matmul(hidden_in, qkv_weight) + qkv_bias).astype(jnp.bfloat16)
     contexts, extended, received = [], [], []
     for pair in range(pairs):
         context, queries = attend_forward(lengths, qkv, pair)
         contexts.append(context)
         extended.append(queries)
-        received.append(exchange(spread(context)))
-    context_all = jnp.concatenate([received[p][s] for s in range(ranks) for p in range(pairs)], axis=1)
+        blocks = spread(context)
+        if pair == 0:
+            first_parts, qkv, blocks, later_part = tie(first_parts, qkv, blocks, later_part)
+            first_rows = gathered(first_parts)
+            later_parts = others(later_part)
+            blocks = [jnp.concatenate([b, inner_bias.reshape(-1, PAIR)]) for b in blocks]
+        if pair == pairs - 1:
+            later_parts, blocks = tie(later_parts, blocks)
+            outer_rest = gathered(later_parts[..., :units])
+            qkv_rest = gathered(later_parts[..., units:])
+        received.append(exchange(blocks))
+    inner_biases = [r[share_rows:].reshape(-1) for r in received[0]]
+    received[0] = [r[:share_rows] for r in received[0]]
+    context_all = jnp.concatenate(
+        [received[p][s] for s in range(ranks) for p in range(pairs)], axis=1
+    )
+    inner_weights = [inner_weight] + [first_rows[s][:, :units] for s in range(ranks - 1)]
+    output_weight_all = jnp.concatenate(
+        [output_weight] + [first_rows[s][:, units:] for s in range(ranks - 1)], axis=1
+    )
+    outer_weights = [outer_weight] + [outer_rest[s] for s in range(ranks - 1)]
+    qkv_weights = [qkv_weight] + [qkv_rest[s] for s in range(ranks - 1)]
 
     hidden_own = take_own(hidden_in).astype(jnp.float32)
     attention = times_rows(context_all, output_weight_all)
@@ -353,12 +417,18 @@
     )
     second_grad = norm_back(final_grad, normal_two, inverse_two, second_gain)
     branch_low = second_grad.astype(jnp.bfloat16)
-    outer_whole = over_rows(branch_low, jnp.concatenate(activated, axis=1)).astype(jnp.bfloat16)
+    activated_all = jnp.concatenate(activated, axis=1)
+    outer_give = first_give(branch_low, activated_all)
+    outer_give, branch_low = tie(outer_give, branch_low)
+    outer_come = flip(outer_give, "dp", 1)
     inner_lows = []
     normed_grad = second_grad
     for s in range(ranks):
         inner_low = (matmul(branch_low, outer_weights[s]) * slopes[s]).astype(jnp.bfloat16)
         inner_lows.append(inner_low)
+        if s == 0:
+            outer_kept = first_keep(branch_low, activated_all, outer_come)
+            inner_low, outer_kept = tie(inner_low, outer_kept)
         normed_grad = normed_grad + times_rows(inner_low, inner_weights[s])
     first_grad = norm_back(normed_grad, normal_one, inverse_one, first_gain)
     attention_low = first_grad.astype(jnp.bfloat16)
@@ -369,71 +439,48 @@
         context_grad = lax.dynamic_update_slice_in_dim(
             context_grad, grads[s], (rank ^ s) * share_rows, 0
         )
-
     inner_low_all = jnp.concatenate(inner_lows, axis=1)
     inner_whole = over_rows(normed_low, inner_low_all).astype(jnp.bfloat16)
     output_whole = over_rows(attention_low, context_all).astype(jnp.bfloat16)
-
-    def reduce_copies(whole):
-        rows = whole.shape[0] // copies
-        bits = [1]
-        while 2 * bits[0] < copies:
-            bits.insert(0, 2 * bits[0])
-        bits = [1] + bits[:-1]
-        blocks = whole.reshape(copies, rows, -1)
-        left = list(range(copies.bit_length() - 1))
-        for bit in bits:
-            place = bit.bit_length() - 1
-            low = 1
-            for p in left:
-                low *= 2 if p < place else 1
-            left.remove(place)
-            blocks = blocks.reshape(-1, 2, low, rows, blocks.shape[-1])
-            mine = (copy >> place) & 1
-            keep = lax.dynamic_index_in_dim(blocks, mine, 1, keepdims=False)
-            give = lax.dynamic_index_in_dim(blocks, 1 - mine, 1, keepdims=False)
-            come = flip(give, "dp", bit)
-            blocks = (keep.astype(jnp.float32) + come.astype(jnp.float32)).astype(jnp.bfloat16)
-            blocks = blocks.reshape(-1, rows, blocks.shape[-1])
-        return blocks[0]
-
-    def scatter_copies(whole):
-        return lax.psum_scatter(whole, "dp", scatter_dimension=0, tiled=True)
-
-    def reduce_ranks(blocks):
-        return sum(g.astype(jnp.float32) for g in exchange(blocks))
-
-    context_grad, outer_whole, inner_whole, output_whole = lax.optimization_barrier(
-        (context_grad, outer_whole, inner_whole, output_whole)
-    )
-    outer_rows = scatter_copies(outer_whole)
-    outer_weight_grad = reduce_ranks(jnp.split(outer_rows, ranks, axis=1))
-    both_rows = reduce_copies(jnp.concatenate([inner_whole, output_whole], axis=1))
-    inner_rows = jnp.split(both_rows[:, : ranks * units], ranks, axis=1)
-    output_rows = jnp.split(both_rows[:, ranks * units :], ranks, axis=1)
-    both_sum = reduce_ranks(
-        [jnp.concatenate([i, o], axis=1) for i, o in zip(inner_rows, output_rows)]
-    )
-    inner_weight_grad, output_weight_grad = both_sum[:, :units], both_sum[:, units:]
+    outer_rows = high_steps(outer_kept)
+    context_grad, inner_whole, output_whole = tie(context_grad, inner_whole, output_whole)
+    inner_rows = scatter_copies(inner_whole)
 
     input_rows = first_grad
-    qkv_sums, query_sums = [], []
+    query_sums = []
     for pair in range(pairs):
         qkv_low = attend_backward(lengths, extended[pair], qkv, contexts[pair], context_grad, pair)
+        blocks = spread(qkv_low)
+        qkv_whole = over_rows(hidden_in, qkv_low).astype(jnp.bfloat16)
+        if pair == 0:
+            blocks, context_grad, outer_rows, qkv_whole = tie(
+                blocks, context_grad, outer_rows, qkv_whole
+            )
+            both = scatter_copies(jnp.concatenate([output_whole, qkv_whole], axis=1))
+            output_rows, qkv_sums = both[:, :model_width], [both[:, model_width:]]
+            outer_weight_grad = reduce_ranks(jnp.split(outer_rows, ranks, axis=1))
+        else:
+            blocks, qkv_low = tie(blocks, qkv_low)
+            come = flip(first_give(hidden_in, qkv_low), "dp", 1)
+            qkv_sums.append(high_steps(first_keep(hidden_in, qkv_low, come)))
         columns = slice(3 * PAIR * pair, 3 * PAIR * (pair + 1))
-        for block, weight in zip(exchange(spread(qkv_low)), qkv_weights):
+        for block, weight in zip(exchange(blocks), qkv_weights):
             input_rows = input_rows + times_rows(block, weight[:, columns])
-        whole = over_rows(hidden_in, qkv_low).astype(jnp.bfloat16)
-        qkv_sums.append(scatter_copies(whole) if pair == 0 else reduce_copies(whole))
-        query_sums.append(jnp.sum(qkv_low[:, :PAIR].astype(jnp.float32), axis=0))
+        query_sums.append(column_sums(qkv_low[:, :PAIR]))
+    inner_parts = jnp.split(inner_rows, ranks, axis=1)
+    output_parts = jnp.split(output_rows, ranks, axis=1)
+    both_sum = reduce_ranks(
+        [jnp.concatenate([i, o], axis=1) for i, o in zip(inner_parts, output_parts)]
+    )
+    inner_weight_grad, output_weight_grad = both_sum[:, :units], both_sum[:, units:]
     qkv_sums = [jnp.split(w.astype(jnp.float32), 3, axis=1) for w in qkv_sums]
     query_weight_grad, key_weight_grad, value_weight_grad = [
         jnp.concatenate([w[i] for w in qkv_sums], axis=1) for i in range(3)
     ]
 
-    def column_sums(array_in):
-        return jnp.sum(array_in.astype(jnp.float32), axis=0)
-
+    query_sums = lax.dynamic_update_slice_in_dim(
+        jnp.zeros((model_width,), jnp.float32), jnp.concatenate(query_sums), rank * heads_width, 0
+    )
     vectors = [
         ordered(column_sums(inner_low_all)),
         column_sums(attention_low),
@@ -443,10 +490,10 @@
         column_sums(final_grad * normal_two),
         column_sums(final_grad),
         ordered(column_sums(grad_all)),
+        query_sums,
         jnp.full((model_width,), loss_part),
     ]
-    vectors = jnp.concatenate(vectors).reshape(-1, model_width)
-    vectors = jnp.sum(lax.all_gather(vectors, ("dp", "tensor")), axis=0)
+    vectors = total(jnp.concatenate(vectors).reshape(-1, model_width), ("dp", "tensor"))
     wide = ranks * units // model_width
     inner_bias_grad = vectors[:wide].reshape(-1)
     (
@@ -457,14 +504,11 @@
         second_gain_grad,
         second_shift_grad,
         value_bias_grad,
-    ) = [vectors[wide + i] for i in range(7)]
-    query_bias_grad = lax.dynamic_update_slice_in_dim(
-        jnp.zeros((model_width,), jnp.float32), jnp.concatenate(query_sums), rank * heads_width, 0
-    )
-    query_bias_grad = total(query_bias_grad, ("dp", "tensor"))
+        query_bias_grad,
+    ) = [vectors[wide + i] for i in range(8)]
     return (
         final.astype(jnp.bfloat16),
-        vectors[wide + 7, 0] / token_total,
+        vectors[wide + 8, 0] / token_total,
         input_rows,
         query_weight_grad,
         query_bias_grad,

time: 584 us -> 546 us (0.935); the launches traced: 573 us -> 542 us
  waiting for transfers between devices: 190 us -> 139 us
  local copies, waits for them, and re-layouts: 67.5 us -> 97.3 us
  other arithmetic: 37.3 us -> 25 us
  matrix products: 96.6 us -> 105 us
    ppermute x47 -> x45, waiting for transfers between devices: 190 us -> 137 us  [flip(): lax.ppermute(array_in, axis_name, [(i, i ^ bits) for i in range(size)])]
    reshape x0 -> x3, local copies, waits for them, and re-layouts: none -> 14.4 us  [the longest x2 14.3 us: half_columns(): blocks = array_in.reshape(array_in.shape[0], copies // 2, 2, -1)]
    dynamic_slice x5 -> x6, local copies, waits for them, and re-layouts: 3.04 us -> 12.6 us  [the longest x3 10.4 us: half_columns(): mine = lax.dynamic_index_in_dim(blocks, copy & 1 ^ other, 2, keepdims=False)]
    dot_general x5 -> x7, matrix products: 28.6 us -> 35.4 us  [over_rows(): lax.dot_general(former, latter, (((0,), (0,)), ((), ())), preferred_eleme...]
    unnamed x192, local copies, waits for them, and re-layouts: 28.8 us -> 35.6 us
    dot_general x10, matrix products: 24.9 us -> 31.6 us  [matmul(): return jnp.dot(former, latter, preferred_element_type=jnp.float32)]
    ppermute x47 -> x45, starting transfers between devices: 70.6 us -> 65 us  [flip(): lax.ppermute(array_in, axis_name, [(i, i ^ bits) for i in range(size)])]
    squeeze x6 -> x9, local copies, waits for them, and re-layouts: 14 us -> 11 us  [the longest x1 5.11 us: shards(): qkv_weights = [qkv_weight] + [qkv_rest[s] for s in range(ranks - 1)]]
  transfers between devices with their start and end apart: 53 -> 50, of which waited for: 18 -> 20; matrix products, arithmetic and copies ran while one was open for 32% -> 39% of each run, Pallas kernels for 16% -> 17%
where the time goes in v3:
time: 546 us; the launch traced here: 542 us
  waiting for transfers between devices  139 us (25%)
  matrix products  105 us (19%)
  local copies, waits for them, and re-layouts  97.3 us (18%)
  Pallas kernels  90.2 us (17%)
  starting transfers between devices  65.5 us (12%)
  other arithmetic  25 us (5%)
  between operations  20 us (4%)
    ppermute x45, waiting for transfers between devices, flip(): lax.ppermute(array_in, axis_name, [(i, i ^ bits) for i in range(size)])  137 us
    ppermute x45, starting transfers between devices, flip(): lax.ppermute(array_in, axis_name, [(i, i ^ bits) for i in range(size)])  65 us
    pallas_call x2, Pallas kernels, attend_backward(): pl.pallas_call(backward_kernel, grid_spec=pltpu.PrefetchScalarGridSpec(nu...  57.7 us
    dot_general x17, matrix products, times_rows(): lax.dot_general(former, latter, (((1,), (1,)), ((), ())), preferred_eleme...  37.6 us
    unnamed x192, local copies, waits for them, and re-layouts  35.6 us
    dot_general x7, matrix products, over_rows(): lax.dot_general(former, latter, (((0,), (0,)), ((), ())), preferred_eleme...  35.4 us
    pallas_call x2, Pallas kernels, attend_forward(): pl.pallas_call(forward_kernel, grid_spec=pltpu.PrefetchScalarGridSpec(num...  32.5 us
    dot_general x10, matrix products, matmul(): return jnp.dot(former, latter, preferred_element_type=jnp.float32)  31.6 us
  transfers between devices with their start and end apart: 50, of which 20 were waited for; matrix products, arithmetic and copies ran while one was open for 39% of the time, Pallas kernels for 17%

profile of v3, /device:TPU:0, one launch (start us, length us, event | category | flops | bytes accessed | tf_op | source)
XLA Modules:
  0.0 542.2 jit_solution(4108149378170467207)
XLA Ops:
  8.4 5.1 collective-permute-start.2
  27.9 16.3 %attend_forward.2 = (bf16[2048,128]{1,0:T(8,128)(2,1)}, bf16[2,2048,128]{2,1,0:T(8,128)(2,1)}) custom-call(s32[1]{0:T(128)} %copy.115.length_ref, bf16[2048,768]{1,0:T(8,128)(2,1)} %fusion.q_ref.k_ref.v_ref, bf16[2048,768]{1,0:T(8,128)(2,1)} %fusion.q_ref.k_ref.v_ref, bf16[2048,768]{1,0:T(8,128)(2,1)} %fusion.q_ref.k_ref.v_ref), custom_call_target="tpu_custom_call" | custom-call | flops 8589934592 | bytes 3145728 | tf_op jit(solution)/shard_map/attend_forward/pallas_call | solution.py:114
  51.9 16.2 %attend_forward.3 = (bf16[2048,128]{1,0:T(8,128)(2,1)}, bf16[2,2048,128]{2,1,0:T(8,128)(2,1)}) custom-call(s32[1]{0:T(128)} %copy.115.length_ref, bf16[2048,768]{1,0:T(8,128)(2,1)} %fusion.q_ref.k_ref.v_ref, bf16[2048,768]{1,0:T(8,128)(2,1)} %fusion.q_ref.k_ref.v_ref, bf16[2048,768]{1,0:T(8,128)(2,1)} %fusion.q_ref.k_ref.v_ref), custom_call_target="tpu_custom_call" | custom-call | flops 8589934592 | bytes 3145728 | tf_op jit(solution)/shard_map/attend_forward/pallas_call | solution.py:114
  69.3 20.2 %collective-permute-done.4 = bf16[128,1792]{1,0:T(8,128)(2,1)S(1)} collective-permute-done((bf16[128,1792]{1,0:T(8,128)(2,1)S(1)}, bf16[128,1792]{1,0:T(8,128)(2,1)S(1)}, u32[]{:S(2)}, u32[]{:S(2)}) %collective-permute-start.4) | collective-permute-done | bytes 458784 | tf_op jit(solution)/shard_map/ppermute | solution.py:242
  105.6 5.4 collective-permute-done.8
  157.5 5.3 multiply_reduce_fusion
  164.7 12.8 %reshape.270 = bf16[512,4,2,128]{3,2,1,0:T(2,128)(2,1)} reshape(bf16[512,1024]{1,0:T(8,128)(2,1)S(1)} %fusion.90) | data formatting | bytes 2097152 | tf_op jit(solution)/shard_map/reshape | solution.py:324
  184.3 6.7 %convolution_convert_fusion.1 = bf16[512,4096]{1,0:T(8,128)(2,1)} fusion(bf16[512,512]{0,1:T(8,128)(2,1)} %bitcast.171, bf16[512,1024]{1,0:T(8,128)(2,1)} %get-tuple-element.195, bf16[512,1024]{1,0:T(8,128)(2,1)} %get-tuple-element.197, bf16[512,1024]{1,0:T(8,128)(2,1)} %get-tuple-element.199, bf16[512,1024]{1,0:T(8,128)(2,1)} %copy-done.72), kind=kOutput, calls=%fused_computation.4 | convolution fusion | flops 2166358016 | bytes 8912896 | tf_op jit(solution)/shard_map/dot_general | solution.py:27
  224.3 7.9 %convolution_convert_fusion = bf16[1024,4096]{1,0:T(8,128)(2,1)} fusion(bf16[512,1024]{1,0:T(8,128)(2,1)S(1)} %copy-done.38, bf16[512,1024]{1,0:T(8,128)(2,1)S(1)} %copy-done.46, bf16[512,1024]{1,0:T(8,128)(2,1)S(1)} %copy-done.48, bf16[512,1024]{1,0:T(8,128)(2,1)S(1)} %multiply_convert_fusion.2, bf16[512,1024]{1,0:T(8,128)(2,1)S(1)} %multiply_convert_fusion.3), kind=kOutput, calls=%fused_computation.2 | convolution fusion | flops 4315938816 | bytes 13631488 | tf_op jit(solution)/shard_map/dot_general | solution.py:27
  232.3 6.1 %add_convert_fusion = bf16[512,4096]{1,0:T(8,128)(2,1)S(1)} fusion(bf16[512,4096]{1,0:T(8,128)(2,1)} %collective-permute-done.15, bf16[512,512]{0,1:T(8,128)(2,1)} %bitcast.170, bf16[512,1024]{1,0:T(8,128)(2,1)} %get-tuple-element.195, bf16[512,1024]{1,0:T(8,128)(2,1)} %get-tuple-element.197, bf16[512,1024]{1,0:T(8,128)(2,1)} %get-tuple-element.199, ...), kind=kOutput, calls=%fused_computation | convolution fusion | flops 2170552320 | bytes 13107200 | tf_op jit(solution)/shard_map/dot_general | solution.py:27
  262.5 8.7 %collective-permute-done.17 = bf16[512,256]{1,0:T(8,128)(2,1)S(1)} collective-permute-done((bf16[512,256]{1,0:T(8,128)(2,1)S(1)}, bf16[512,256]{1,0:T(8,128)(2,1)S(1)}, u32[]{:S(2)}, u32[]{:S(2)}) %collective-permute-start.17) | collective-permute-done | bytes 262176 | tf_op jit(solution)/shard_map/ppermute | solution.py:242
  272.6 28.9 %attend_backward.2 = bf16[2048,384]{1,0:T(8,128)(2,1)} custom-call(s32[1]{0:T(128)} %copy.115.length_ref, bf16[2,2048,128]{2,1,0:T(8,128)(2,1)} %get-tuple-element.70.extended_ref, bf16[2048,768]{1,0:T(8,128)(2,1)} %fusion.q_ref.k_ref.v_ref, bf16[2048,768]{1,0:T(8,128)(2,1)} %fusion.q_ref.k_ref.v_ref, bf16[2048,128]{1,0:T(8,128)(2,1)} %get-tuple-element.53.context_ref, ...), custom_call_target="tpu_custom_call" | custom-call | flops 21474836480 | bytes 5242880 | tf_op jit(solution)/shard_map/attend_backward/pallas_call | solution.py:207
  301.6 5.2 fusion.43
  313.4 6.2 %collective-permute-done.22 = bf16[1,1,128,2048]{3,2,1,0:T(8,128)(2,1)S(1)} collective-permute-done((bf16[1,1,128,2048]{3,2,1,0:T(8,128)(2,1)S(1)}, bf16[1,1,128,2048]{3,2,1,0:T(8,128)(2,1)S(1)}, u32[]{:S(2)}, u32[]{:S(2)}) %collective-permute-start.22) | collective-permute-done | bytes 524320 | tf_op jit(solution)/shard_map/ppermute | solution.py:242
  324.6 6.5 %copy.56 = bf16[2048,1024]{0,1:T(8,128)(2,1)} copy(bf16[2048,1024]{1,0:T(8,128)(2,1)} %param.19) | data formatting | bytes 8388608 | tf_op args[0]
  336.1 5.1 slice_bitcast_fusion.12
  347.8 28.8 %attend_backward.3 = bf16[2048,384]{1,0:T(8,128)(2,1)} custom-call(s32[1]{0:T(128)} %copy.115.length_ref, bf16[2,2048,128]{2,1,0:T(8,128)(2,1)} %get-tuple-element.72.extended_ref, bf16[2048,768]{1,0:T(8,128)(2,1)} %fusion.q_ref.k_ref.v_ref, bf16[2048,768]{1,0:T(8,128)(2,1)} %fusion.q_ref.k_ref.v_ref, bf16[2048,128]{1,0:T(8,128)(2,1)} %get-tuple-element.57.context_ref, ...), custom_call_target="tpu_custom_call" | custom-call | flops 21474836480 | bytes 5242880 | tf_op jit(solution)/shard_map/attend_backward/pallas_call | solution.py:207
  380.6 7.8 %collective-permute-start.32 = (bf16[512,384]{1,0:T(8,128)(2,1)}, bf16[512,384]{1,0:T(8,128)(2,1)}, u32[]{:S(2)}, u32[]{:S(2)}) collective-permute-start(bf16[512,384]{1,0:T(8,128)(2,1)} %get-tuple-element.82), channel_id=1, source_target_pairs={{0,2},{1,3},{2,0},{3,1},{4,6},{5,7},{6,4},{7,5},{8,10},{9,11},{10,... | collective-permute-start | bytes 1179656 | tf_op jit(solution)/shard_map/ppermute | solution.py:242
  403.9 12.1 %collective-permute-done.26 = f32[13,1024]{1,0:T(8,128)S(1)} collective-permute-done((f32[13,1024]{1,0:T(8,128)S(1)}, f32[13,1024]{1,0:T(8,128)S(1)}, u32[]{:S(2)}, u32[]{:S(2)}) %collective-permute-start.26) | collective-permute-done | bytes 53280 | tf_op jit(solution)/shard_map/ppermute | solution.py:242
  419.9 27.9 %collective-permute-done.43 = bf16[128,1024]{1,0:T(8,128)(2,1)S(1)} collective-permute-done((bf16[128,1024]{1,0:T(8,128)(2,1)S(1)}, bf16[128,1024]{1,0:T(8,128)(2,1)S(1)}, u32[]{:S(2)}, u32[]{:S(2)}) %collective-permute-start.43) | collective-permute-done | bytes 262176 | tf_op jit(solution)/shard_map/ppermute | solution.py:242
  451.7 14.1 %collective-permute-done.27 = f32[13,1024]{1,0:T(8,128)S(1)} collective-permute-done((f32[13,1024]{1,0:T(8,128)S(1)}, f32[13,1024]{1,0:T(8,128)S(1)}, u32[]{:S(2)}, u32[]{:S(2)}) %collective-permute-start.27) | collective-permute-done | bytes 53280 | tf_op jit(solution)/shard_map/ppermute | solution.py:242
  482.3 6.2 %collective-permute-done.28 = bf16[512,384]{1,0:T(8,128)(2,1)} collective-permute-done((bf16[512,384]{1,0:T(8,128)(2,1)}, bf16[512,384]{1,0:T(8,128)(2,1)}, u32[]{:S(2)}, u32[]{:S(2)}) %collective-permute-start.28) | collective-permute-done | bytes 393248 | tf_op jit(solution)/shard_map/ppermute | solution.py:242
  511.6 5.8 %collective-permute-done.41 = bf16[128,1280]{1,0:T(8,128)(2,1)S(1)} collective-permute-done((bf16[128,1280]{1,0:T(8,128)(2,1)S(1)}, bf16[128,1280]{1,0:T(8,128)(2,1)S(1)}, u32[]{:S(2)}, u32[]{:S(2)}) %collective-permute-start.41) | collective-permute-done | bytes 327712 | tf_op jit(solution)/shard_map/ppermute | solution.py:242
  517.4 15.2 %collective-permute-done.40 = bf16[128,1280]{1,0:T(8,128)(2,1)S(1)} collective-permute-done((bf16[128,1280]{1,0:T(8,128)(2,1)S(1)}, bf16[128,1280]{1,0:T(8,128)(2,1)S(1)}, u32[]{:S(2)}, u32[]{:S(2)}) %collective-permute-start.40) | collective-permute-done | bytes 327712 | tf_op jit(solution)/shard_map/ppermute | solution.py:242
  (431 shorter events, 241.5 us)
Async XLA Ops:
  7.2 117.6 %all-gather.4.cloned.1.call-start = ((), (), s32[]{:S(2)}) async-start(), calls=%async_computation.2 | async-start | bytes 8847360 | tf_op jit(solution)/shard_map/all_gather | solution.py:302
  8.4 37.9 %collective-permute-start.2 = (bf16[128,1280]{1,0:T(8,128)(2,1)S(1)}, bf16[128,1280]{1,0:T(8,128)(2,1)S(1)}, u32[]{:S(2)}, u32[]{:S(2)}) collective-permute-start(bf16[128,1280]{1,0:T(8,128)(2,1)S(1)} %fusion.73), channel_id=1, source_target_pairs={{0,3},{1,2},{2,1},{3,0},{4,7},{5,6},{6,5},{7,4},{8,11},{9,10},{10,... | collective-permute-start | bytes 983048 | tf_op jit(solution)/shard_map/ppermute | solution.py:242
  13.5 32.8 %collective-permute-start.1 = (bf16[128,1280]{1,0:T(8,128)(2,1)S(1)}, bf16[128,1280]{1,0:T(8,128)(2,1)S(1)}, u32[]{:S(2)}, u32[]{:S(2)}) collective-permute-start(bf16[128,1280]{1,0:T(8,128)(2,1)S(1)} %fusion.73), channel_id=1, source_target_pairs={{0,2},{1,3},{2,0},{3,1},{4,6},{5,7},{6,4},{7,5},{8,10},{9,11},{10,... | collective-permute-start | bytes 983048 | tf_op jit(solution)/shard_map/ppermute | solution.py:242
  13.5 32.8 %collective-permute-start = (bf16[128,1280]{1,0:T(8,128)(2,1)S(1)}, bf16[128,1280]{1,0:T(8,128)(2,1)S(1)}, u32[]{:S(2)}, u32[]{:S(2)}) collective-permute-start(bf16[128,1280]{1,0:T(8,128)(2,1)S(1)} %fusion.73), channel_id=1, source_target_pairs={{0,1},{1,0},{2,3},{3,2},{4,5},{5,4},{6,7},{7,6},{8,9},{9,8},{10,11... | collective-permute-start | bytes 983048 | tf_op jit(solution)/shard_map/ppermute | solution.py:242
  47.4 101.0 %all-gather.6.cloned.1.call-start = ((), (), s32[]{:S(2)}) async-start(), calls=%async_computation.3 | async-start | bytes 7077888 | tf_op jit(solution)/shard_map/all_gather | solution.py:302
  47.5 21.8 %collective-permute-start.5 = (bf16[128,1792]{1,0:T(8,128)(2,1)S(1)}, bf16[128,1792]{1,0:T(8,128)(2,1)S(1)}, u32[]{:S(2)}, u32[]{:S(2)}) collective-permute-start(bf16[128,1792]{1,0:T(8,128)(2,1)S(1)} %constant_dynamic-slice_fusion.30), channel_id=1, source_target_pairs={{0,3},{1,2},{2,1},{3,0},{4,7},{5,6},{6,5},{7,4},{8,11},{9,10},{10,... | collective-permute-start | bytes 1376264 | tf_op jit(solution)/shard_map/ppermute | solution.py:242
  51.3 38.3 %collective-permute-start.4 = (bf16[128,1792]{1,0:T(8,128)(2,1)S(1)}, bf16[128,1792]{1,0:T(8,128)(2,1)S(1)}, u32[]{:S(2)}, u32[]{:S(2)}) collective-permute-start(bf16[128,1792]{1,0:T(8,128)(2,1)S(1)} %constant_dynamic-slice_fusion.30), channel_id=1, source_target_pairs={{0,2},{1,3},{2,0},{3,1},{4,6},{5,7},{6,4},{7,5},{8,10},{9,11},{10,... | collective-permute-start | bytes 1376264 | tf_op jit(solution)/shard_map/ppermute | solution.py:242
  51.3 38.3 %collective-permute-start.3 = (bf16[128,1792]{1,0:T(8,128)(2,1)S(1)}, bf16[128,1792]{1,0:T(8,128)(2,1)S(1)}, u32[]{:S(2)}, u32[]{:S(2)}) collective-permute-start(bf16[128,1792]{1,0:T(8,128)(2,1)S(1)} %constant_dynamic-slice_fusion.30), channel_id=1, source_target_pairs={{0,1},{1,0},{2,3},{3,2},{4,5},{5,4},{6,7},{7,6},{8,9},{9,8},{10,11... | collective-permute-start | bytes 1376264 | tf_op jit(solution)/shard_map/ppermute | solution.py:242
  90.8 245.3 %all-gather.8.cloned.1.call-start = ((), (), s32[]{:S(2)}) async-start(), calls=%async_computation.4 | async-start | bytes 5308416 | tf_op jit(solution)/shard_map/all_gather | solution.py:302
  117.0 384.7 %reduce-scatter.3.cloned.1.call-start = ((), (), s32[]{:S(2)}) async-start(), calls=%async_computation.5 | async-start | bytes 3244032 | tf_op jit(solution)/shard_map/reduce_scatter | solution.py:357
  199.2 33.1 %collective-permute-start.15 = (bf16[512,4096]{1,0:T(8,128)(2,1)}, bf16[512,4096]{1,0:T(8,128)(2,1)}, u32[]{:S(2)}, u32[]{:S(2)}) collective-permute-start(bf16[512,4096]{1,0:T(8,128)(2,1)} %convolution_convert_fusion.1), channel_id=1, source_target_pairs={{0,4},{4,0},{8,12},{12,8},{16,20},{20,16},{24,28},{28,24},{1,5},{5... | collective-permute-start | bytes 12582920 | tf_op jit(solution)/shard_map/ppermute | solution.py:242
  249.8 21.3 %collective-permute-start.17 = (bf16[512,256]{1,0:T(8,128)(2,1)S(1)}, bf16[512,256]{1,0:T(8,128)(2,1)S(1)}, u32[]{:S(2)}, u32[]{:S(2)}) collective-permute-start(bf16[512,256]{1,0:T(8,128)(2,1)S(1)} %get-tuple-element.127), channel_id=1, source_target_pairs={{0,2},{1,3},{2,0},{3,1},{4,6},{5,7},{6,4},{7,5},{8,10},{9,11},{10,... | collective-permute-start | bytes 786440 | tf_op jit(solution)/shard_map/ppermute | solution.py:242
  257.1 49.7 %collective-permute-start.21 = (bf16[2,1,128,2048]{3,2,1,0:T(8,128)(2,1)}, bf16[2,1,128,2048]{3,2,1,0:T(8,128)(2,1)}, u32[]{:S(2)}, u32[]{:S(2)}) collective-permute-start(bf16[2,1,128,2048]{3,2,1,0:T(8,128)(2,1)} %dynamic-slice_bitcast_fusion), channel_id=1, source_target_pairs={{0,8},{4,12},{8,0},{12,4},{16,24},{20,28},{24,16},{28,20},{1,9},{5... | collective-permute-start | bytes 3145736 | tf_op jit(solution)/shard_map/ppermute | solution.py:242
  258.6 51.1 %collective-permute-start.19 = (bf16[1,2,128,2048]{3,2,1,0:T(8,128)(2,1)S(1)}, bf16[1,2,128,2048]{3,2,1,0:T(8,128)(2,1)}, u32[]{:S(2)}, u32[]{:S(2)}) collective-permute-start(bf16[1,2,128,2048]{3,2,1,0:T(8,128)(2,1)S(1)} %dynamic-slice_bitcast_fusion.1), channel_id=1, source_target_pairs={{0,16},{4,20},{8,24},{12,28},{16,0},{20,4},{24,8},{28,12},{1,17},{... | collective-permute-start | bytes 3145736 | tf_op jit(solution)/shard_map/ppermute | solution.py:242
  324.5 179.1 %reduce-scatter.5.cloned.1.call-start = ((), (), s32[]{:S(2)}) async-start(), calls=%async_computation.6 | async-start | bytes 9437184 | tf_op jit(solution)/shard_map/reduce_scatter | solution.py:357
  380.6 92.3 %collective-permute-start.32 = (bf16[512,384]{1,0:T(8,128)(2,1)}, bf16[512,384]{1,0:T(8,128)(2,1)}, u32[]{:S(2)}, u32[]{:S(2)}) collective-permute-start(bf16[512,384]{1,0:T(8,128)(2,1)} %get-tuple-element.82), channel_id=1, source_target_pairs={{0,2},{1,3},{2,0},{3,1},{4,6},{5,7},{6,4},{7,5},{8,10},{9,11},{10,... | collective-permute-start | bytes 1179656 | tf_op jit(solution)/shard_map/ppermute | solution.py:242
  392.8 25.6 %collective-permute-start.44 = (bf16[128,1024]{1,0:T(8,128)(2,1)S(1)}, bf16[128,1024]{1,0:T(8,128)(2,1)S(1)}, u32[]{:S(2)}, u32[]{:S(2)}) collective-permute-start(bf16[128,1024]{1,0:T(8,128)(2,1)S(1)} %get-tuple-element.120), channel_id=1, source_target_pairs={{0,3},{1,2},{2,1},{3,0},{4,7},{5,6},{6,5},{7,4},{8,11},{9,10},{10,... | collective-permute-start | bytes 786440 | tf_op jit(solution)/shard_map/ppermute | solution.py:242
  394.4 53.5 %collective-permute-start.43 = (bf16[128,1024]{1,0:T(8,128)(2,1)S(1)}, bf16[128,1024]{1,0:T(8,128)(2,1)S(1)}, u32[]{:S(2)}, u32[]{:S(2)}) collective-permute-start(bf16[128,1024]{1,0:T(8,128)(2,1)S(1)} %get-tuple-element.121), channel_id=1, source_target_pairs={{0,2},{1,3},{2,0},{3,1},{4,6},{5,7},{6,4},{7,5},{8,10},{9,11},{10,... | collective-permute-start | bytes 786440 | tf_op jit(solution)/shard_map/ppermute | solution.py:242
  394.4 53.5 %collective-permute-start.42 = (bf16[128,1024]{1,0:T(8,128)(2,1)S(1)}, bf16[128,1024]{1,0:T(8,128)(2,1)S(1)}, u32[]{:S(2)}, u32[]{:S(2)}) collective-permute-start(bf16[128,1024]{1,0:T(8,128)(2,1)S(1)} %get-tuple-element.119), channel_id=1, source_target_pairs={{0,1},{1,0},{2,3},{3,2},{4,5},{5,4},{6,7},{7,6},{8,9},{9,8},{10,11... | collective-permute-start | bytes 786440 | tf_op jit(solution)/shard_map/ppermute | solution.py:242
  415.9 63.4 %collective-permute-start.31 = (bf16[512,384]{1,0:T(8,128)(2,1)}, bf16[512,384]{1,0:T(8,128)(2,1)}, u32[]{:S(2)}, u32[]{:S(2)}) collective-permute-start(bf16[512,384]{1,0:T(8,128)(2,1)} %get-tuple-element.81), channel_id=1, source_target_pairs={{0,1},{1,0},{2,3},{3,2},{4,5},{5,4},{6,7},{7,6},{8,9},{9,8},{10,11... | collective-permute-start | bytes 1179656 | tf_op jit(solution)/shard_map/ppermute | solution.py:242
  418.4 72.1 %collective-permute-start.30 = (bf16[512,384]{1,0:T(8,128)(2,1)}, bf16[512,384]{1,0:T(8,128)(2,1)S(1)}, u32[]{:S(2)}, u32[]{:S(2)}) collective-permute-start(bf16[512,384]{1,0:T(8,128)(2,1)} %get-tuple-element.79), channel_id=1, source_target_pairs={{0,3},{1,2},{2,1},{3,0},{4,7},{5,6},{6,5},{7,4},{8,11},{9,10},{10,... | collective-permute-start | bytes 1179656 | tf_op jit(solution)/shard_map/ppermute | solution.py:242
  447.8 28.6 %collective-permute-start.29 = (bf16[512,384]{1,0:T(8,128)(2,1)}, bf16[512,384]{1,0:T(8,128)(2,1)}, u32[]{:S(2)}, u32[]{:S(2)}) collective-permute-start(bf16[512,384]{1,0:T(8,128)(2,1)} %get-tuple-element.78), channel_id=1, source_target_pairs={{0,2},{1,3},{2,0},{3,1},{4,6},{5,7},{6,4},{7,5},{8,10},{9,11},{10,... | collective-permute-start | bytes 1179656 | tf_op jit(solution)/shard_map/ppermute | solution.py:242
  505.1 27.5 %collective-permute-start.40 = (bf16[128,1280]{1,0:T(8,128)(2,1)S(1)}, bf16[128,1280]{1,0:T(8,128)(2,1)S(1)}, u32[]{:S(2)}, u32[]{:S(2)}) collective-permute-start(bf16[128,1280]{1,0:T(8,128)(2,1)S(1)} %pad_maximum_fusion.15), channel_id=1, source_target_pairs={{0,2},{1,3},{2,0},{3,1},{4,6},{5,7},{6,4},{7,5},{8,10},{9,11},{10,... | collective-permute-start | bytes 983048 | tf_op jit(solution)/shard_map/ppermute | solution.py:242
  509.4 23.3 %collective-permute-start.39 = (bf16[128,1280]{1,0:T(8,128)(2,1)S(1)}, bf16[128,1280]{1,0:T(8,128)(2,1)S(1)}, u32[]{:S(2)}, u32[]{:S(2)}) collective-permute-start(bf16[128,1280]{1,0:T(8,128)(2,1)S(1)} %pad_maximum_fusion.14), channel_id=1, source_target_pairs={{0,1},{1,0},{2,3},{3,2},{4,5},{5,4},{6,7},{7,6},{8,9},{9,8},{10,11... | collective-permute-start | bytes 983048 | tf_op jit(solution)/shard_map/ppermute | solution.py:242
  (104 other events, 638.3 us)
Sparse Core Ops, SparseCore 0:
  47.6 53.4 all-gather.3
  102.9 45.4 all-gather.5
  150.3 38.7 all-gather.7
  324.6 48.7 reduce-scatter.2
  376.7 71.5 reduce-scatter.4
